TPU v7x, 512 devices: a whole 4x8x8 slice. The times are simulated.
512 devices in a mesh: dp: 8 (over y), pipe: 4 (over z_lo), tensor: 16 (over z_hi, x, core).
Axes of the slice: x: 4, y: 8, z: 8 (z_hi: 2, z_lo: 4; z = z_hi * 4 + z_lo), core: 2. Of those that a mesh axis runs over, the one named last changes fastest.
Arguments:
- activations: bfloat16 [4, 1536, 4096], P('pipe', 'tensor', 'dp'), may hold values from -6 to 6
- upstream: bfloat16 [4, 1536, 4096], P('pipe', 'tensor', 'dp'), may hold values from -4 to 4
- gate_value: bfloat16 [4, 1536, 14336], P('pipe', 'dp', 'tensor'), may hold values from -6 to 6
- up_value: bfloat16 [4, 1536, 14336], P('pipe', 'dp', 'tensor'), may hold values from -6 to 6
- hidden_grad: bfloat16 [4, 1536, 14336], P('pipe', 'dp', 'tensor'), may hold values from -4 to 4
- gate_weight: bfloat16 [4, 4096, 14336], P('pipe', 'dp', 'tensor'), may hold values from -0.09375 to 0.09375
- up_weight: bfloat16 [4, 4096, 14336], P('pipe', 'dp', 'tensor'), may hold values from -0.09375 to 0.09375
- gate_mask: int32 [4, 32, 112], P('pipe', 'dp', 'tensor'), may hold values 0 or 1
- up_mask: int32 [4, 32, 112], P('pipe', 'dp', 'tensor'), may hold values 0 or 1
Outputs:
- gate_gradient: bfloat16 [4, 4096, 14336], P('pipe', 'dp', 'tensor')
- up_gradient: bfloat16 [4, 4096, 14336], P('pipe', 'dp', 'tensor')
- handed_back: bfloat16 [4, 1536, 4096], P('pipe', 'tensor', 'dp')
Inputs may be any that keep to these rules, and one draw needn't show every extreme that they name: gate_mask[s, i, j] keeps (1) or prunes (0) block (i, j) of gate_weight[s]. up_mask[s, i, j] keeps (1) or prunes (0) block (i, j) of up_weight[s].
All inputs are finite; a program needn't handle non-finite values.
Results may differ from a plain program's by a relative error of at most 0.0049.
Values may be sent and summed in bfloat16 or wider, within the bound.
A program may use at most 64 MiB of HBM per device.

v0:
```python
import jax
import jax.numpy as jnp
from jax import lax
from jax.sharding import PartitionSpec as P


def shifted(array, axis, by):
    devices = lax.axis_size(axis)
    pairs = [(i, i + by) for i in range(devices) if 0 <= i + by < devices]
    return lax.ppermute(array, axis, pairs)


def apply_blocks(matrix, keep_mask):
    rows_blocks, cols_blocks = keep_mask.shape
    shaped = matrix.reshape(
        rows_blocks, matrix.shape[0] // rows_blocks, cols_blocks, matrix.shape[1] // cols_blocks
    )
    return (shaped * keep_mask.astype(matrix.dtype)[:, None, :, None]).reshape(matrix.shape)


def per_device(
    activations,
    upstream,
    gate_value,
    up_value,
    hidden_grad,
    gate_weight,
    up_weight,
    gate_mask,
    up_mask,
):
    gathered = lax.all_gather(activations, "tensor", axis=1, tiled=True)[0]
    gate_float = gate_value[0].astype(jnp.float32)
    up_float = up_value[0].astype(jnp.float32)
    hidden_float = hidden_grad[0].astype(jnp.float32)
    gate_sigmoid = jax.nn.sigmoid(gate_float)
    up_delta = (hidden_float * gate_float * gate_sigmoid).astype(jnp.bfloat16)
    gate_delta = (
        hidden_float * up_float * gate_sigmoid * (1.0 + gate_float * (1.0 - gate_sigmoid))
    ).astype(jnp.bfloat16)
    gate_kept = apply_blocks(gate_weight[0], gate_mask[0])
    up_kept = apply_blocks(up_weight[0], up_mask[0])
    over_tokens = (((0,), (0,)), ((), ()))
    over_hidden = (((1,), (1,)), ((), ()))
    gate_piece = lax.all_gather(gate_delta, "dp", axis=0, tiled=True)
    up_piece = lax.all_gather(up_delta, "dp", axis=0, tiled=True)
    gate_acc = lax.dot_general(
        gathered, gate_piece, over_tokens, preferred_element_type=jnp.float32
    )
    up_acc = lax.dot_general(gathered, up_piece, over_tokens, preferred_element_type=jnp.float32)
    partial_rows = lax.dot_general(
        gate_piece, gate_kept, over_hidden, preferred_element_type=jnp.float32
    )
    partial_rows = partial_rows + lax.dot_general(
        up_piece, up_kept, over_hidden, preferred_element_type=jnp.float32
    )
    branch = partial_rows
    gate_acc, up_acc, branch = (gate_acc, up_acc, branch)
    own_rows = lax.psum_scatter(branch, "tensor", scatter_dimension=0, tiled=True)
    gate_gradient = apply_blocks(gate_acc, gate_mask[0]).astype(jnp.bfloat16)[None]
    up_gradient = apply_blocks(up_acc, up_mask[0]).astype(jnp.bfloat16)[None]
    section_grad = (upstream[0].astype(jnp.float32) + own_rows).astype(jnp.bfloat16)
    handed = shifted(section_grad, "pipe", -1)
    return (gate_gradient, up_gradient, handed[None])


def solution(mesh):
    return jax.shard_map(
        per_device,
        mesh=mesh,
        in_specs=(
            P("pipe", "tensor", "dp"),
            P("pipe", "tensor", "dp"),
            P("pipe", "dp", "tensor"),
            P("pipe", "dp", "tensor"),
            P("pipe", "dp", "tensor"),
            P("pipe", "dp", "tensor"),
            P("pipe", "dp", "tensor"),
            P("pipe", "dp", "tensor"),
            P("pipe", "dp", "tensor"),
        ),
        out_specs=(P("pipe", "dp", "tensor"), P("pipe", "dp", "tensor"), P("pipe", "tensor", "dp")),
        check_vma=False,
    )
```

profile of v0, /device:TPU:6, one launch (start us, length us, event | category | flops | bytes accessed | tf_op | source)
XLA Modules:
  0.0 296.3 jit_solution(10414191053938637605)
XLA Ops:
  7.2 0.0 copy-start
  7.2 0.0 copy-start.3
  7.2 0.0 copy-start.1
  7.2 0.0 all-gather.4.cloned.1.call-start
  7.2 2.5 fusion.29
  9.8 0.0 all-gather.4.cloned.1.call-update
  9.8 0.0 all-gather.8.cloned.1.call-start
  9.8 0.7 all-gather.8.cloned.1.call-update
  10.5 0.0 all-gather.6.cloned.1.call-start
  10.6 0.7 all-gather.6.cloned.1.call-update
  11.3 0.0 reduce-scatter.2.cloned.1.call-start
  11.3 0.8 convert_bitcast_fusion.3
  12.1 0.1 copy.19
  12.2 0.0 copy-done
  12.2 0.5 copy.18
  12.7 0.0 copy-done.3
  12.7 0.1 copy.21
  12.8 0.0 copy-done.1
  12.9 0.5 copy.20
  13.4 47.5 %all-gather.4.cloned.1.call-done = bf16[1536,896]{1,0:T(8,128)(2,1)} async-done(((bf16[192,896]{1,0:T(8,128)(2,1)}), bf16[1536,896]{1,0:T(8,128)(2,1)}) %all-gather.4.cloned.1.call-update) | async-done | bytes 2752528 | tf_op jit(solution)/shard_map/all_gather | solution.py:45
  60.9 0.3 mul.74
  61.2 5.3 %fusion.17 = f32[1536,512]{1,0:T(8,128)} fusion(bf16[1536,896]{1,0:T(8,128)(2,1)} %all-gather.4.cloned.1.call-done, bf16[112,8,4,128]{3,2,1,0:T(4,128)(2,1)S(1)} %bitcast.99, bf16[1,512,896]{1,2,0:T(8,128)(2,1)S(1)} %copy.18), kind=kOutput, calls=%fused_computation.17 | convolution fusion | flops 1409744896 | bytes 7733248 | tf_op jit(solution)/shard_map/dot_general | solution.py:51
  66.5 41.5 %all-gather.8.cloned.1.call-done = bf16[1536,896]{1,0:T(8,128)(2,1)} async-done(((bf16[192,896]{1,0:T(8,128)(2,1)}), bf16[1536,896]{1,0:T(8,128)(2,1)}) %all-gather.8.cloned.1.call-update) | async-done | bytes 2752528 | tf_op jit(solution)/shard_map/all_gather | solution.py:46
  108.0 0.3 mul.77
  108.3 6.2 %convolution_add_fusion = f32[1536,512]{1,0:T(8,128)} fusion(f32[1536,512]{1,0:T(8,128)} %fusion.17, bf16[1536,896]{1,0:T(8,128)(2,1)} %all-gather.8.cloned.1.call-done, bf16[112,8,4,128]{3,2,1,0:T(4,128)(2,1)S(1)} %bitcast.98, bf16[1,512,896]{1,2,0:T(8,128)(2,1)S(1)} %copy.20), kind=kOutput, calls=%fused_computation | convolution fusion | flops 1410531328 | bytes 10878976 | tf_op jit(solution)/shard_map/dot_general | solution.py:54
  114.5 0.0 reduce-scatter.2.cloned.1.call-update
  114.5 0.1 copy.16
  114.6 0.1 copy.17
  114.7 60.2 %all-gather.6.cloned.1.call-done = bf16[1,1536,512]{2,1,0:T(8,128)(2,1)} async-done(((bf16[1,96,512]{2,1,0:T(8,128)(2,1)}), bf16[1,1536,512]{2,1,0:T(8,128)(2,1)}) %all-gather.6.cloned.1.call-update) | async-done | bytes 1572880 | tf_op jit(solution)/shard_map/all_gather | solution.py:32
  174.9 0.3 mul.66
  175.2 0.0 copy-start.2
  175.3 3.9 %fusion.10 = bf16[1,512,896]{1,2,0:T(8,128)(2,1)S(1)} fusion(f32[112,8,4,128]{3,2,1,0:T(4,128)S(1)} %bitcast.97, bf16[1536,896]{1,0:T(8,128)(2,1)} %all-gather.4.cloned.1.call-done, bf16[1,1536,512]{2,1,0:T(8,128)(2,1)} %all-gather.6.cloned.1.call-done), kind=kOutput, calls=%fused_computation.9 | convolution fusion | flops 1410203648 | bytes 7077888 | tf_op jit(solution)/shard_map/dot_general | solution.py:47
  179.1 101.0 %reduce-scatter.2.cloned.1.call-done = f32[96,512]{1,0:T(8,128)} async-done(((f32[1536,512]{1,0:T(8,128)}), f32[96,512]{1,0:T(8,128)}) %reduce-scatter.2.cloned.1.call-update) | async-done | bytes 196624 | tf_op jit(solution)/shard_map/reduce_scatter | solution.py:59
  280.1 0.0 copy-done.2
  280.1 0.9 fusion.30
  281.1 1.3 collective-permute-start
  282.4 0.3 mul.71
  282.7 3.9 %fusion.13 = bf16[1,512,896]{1,2,0:T(8,128)(2,1)S(1)} fusion(f32[112,8,4,128]{3,2,1,0:T(4,128)S(1)} %bitcast.96, bf16[1536,896]{1,0:T(8,128)(2,1)} %all-gather.8.cloned.1.call-done, bf16[1,1536,512]{2,1,0:T(8,128)(2,1)} %all-gather.6.cloned.1.call-done), kind=kOutput, calls=%fused_computation.10 | convolution fusion | flops 1410203648 | bytes 7077888 | tf_op jit(solution)/shard_map/dot_general | solution.py:50
  286.6 1.3 copy.22
  287.8 1.3 copy.23
  289.1 0.0 collective-permute-done
  289.1 0.6 copy.43
  (1 shorter events, 0.0 us)
Async XLA Ops:
  7.2 5.0 %copy-start = (bf16[1,512,896]{2,1,0:T(8,128)(2,1)S(1)}, bf16[1,512,896]{2,1,0:T(8,128)(2,1)}, u32[]{:S(2)}) copy-start(bf16[1,512,896]{2,1,0:T(8,128)(2,1)} %param.14) | copy-start | bytes 2752516
  7.2 5.5 %copy-start.3 = (s32[1,4,7]{2,1,0:T(4,128)S(1)}, s32[1,4,7]{2,1,0:T(4,128)}, u32[]{:S(2)}) copy-start(s32[1,4,7]{2,1,0:T(4,128)} %param.17) | copy-start | bytes 340
  7.2 5.7 %copy-start.1 = (bf16[1,512,896]{2,1,0:T(8,128)(2,1)S(1)}, bf16[1,512,896]{2,1,0:T(8,128)(2,1)}, u32[]{:S(2)}) copy-start(bf16[1,512,896]{2,1,0:T(8,128)(2,1)} %param.15) | copy-start | bytes 2752516
  7.2 53.7 %all-gather.4.cloned.1.call-start = ((), (), s32[]{:S(2)}) async-start(), calls=%async_computation.1 | async-start | bytes 3096576 | tf_op jit(solution)/shard_map/all_gather | solution.py:45
  9.8 98.2 %all-gather.8.cloned.1.call-start = ((), (), s32[]{:S(2)}) async-start(), calls=%async_computation.3 | async-start | bytes 3096576 | tf_op jit(solution)/shard_map/all_gather | solution.py:46
  10.5 164.4 %all-gather.6.cloned.1.call-start = ((), (), s32[]{:S(2)}) async-start(), calls=%async_computation.2 | async-start | bytes 1671168 | tf_op jit(solution)/shard_map/all_gather | solution.py:32
  11.3 268.9 %reduce-scatter.2.cloned.1.call-start = ((), (), s32[]{:S(2)}) async-start(), calls=%async_computation.4 | async-start | bytes 3342336 | tf_op jit(solution)/shard_map/reduce_scatter | solution.py:59
  175.2 104.9 %copy-start.2 = (bf16[1,96,512]{2,1,0:T(8,128)(2,1)S(1)}, bf16[1,96,512]{2,1,0:T(8,128)(2,1)}, u32[]{:S(2)}) copy-start(bf16[1,96,512]{2,1,0:T(8,128)(2,1)} %param.10) | copy-start | bytes 294916
  281.1 8.0 %collective-permute-start = (bf16[96,512]{1,0:T(8,128)(2,1)S(1)}, bf16[96,512]{1,0:T(8,128)(2,1)S(1)}, u32[]{:S(2)}, u32[]{:S(2)}) collective-permute-start(bf16[96,512]{1,0:T(8,128)(2,1)S(1)} %fusion.30), channel_id=1, source_target_pairs={{16,0},{32,16},{48,32},{17,1},{33,17},{49,33},{18,2},{34,18},{50,3... | collective-permute-start | bytes 294920 | tf_op jit(solution)/shard_map/ppermute | solution.py:10
Sparse Core Ops, SparseCore 0:
  10.7 50.1 all-gather.3
  63.6 44.3 all-gather.7
  111.3 63.5 all-gather.5
  179.7 100.4 reduce-scatter.1
where the time goes:
time: 297 us; the launch traced here: 296 us
  waiting for transfers between devices  252 us (85%)
  matrix products  19.2 us (6%)
  between operations  13.9 us (5%)
  local copies, waits for them, and re-layouts  5.86 us (2%)
  other arithmetic  4.23 us (1%)
    reduce_scatter x1, waiting for transfers between devices, per_device(): lax.psum_scatter(branch, 'tensor', scatter_dimension=0, tiled=True)  101 us
    all_gather x1, waiting for transfers between devices, per_device(): gathered = lax.all_gather(activations, 'tensor', axis=1, tiled=True)[0]  60.2 us
    all_gather x1, waiting for transfers between devices, per_device(): gate_piece = lax.all_gather(gate_delta, 'dp', axis=0, tiled=True)  47.5 us
    all_gather x1, waiting for transfers between devices, per_device(): up_piece = lax.all_gather(up_delta, 'dp', axis=0, tiled=True)  41.5 us
    dot_general x1, matrix products, per_device(): lax.dot_general(up_piece, up_kept, over_hidden, preferred_element_type=jn...  6.21 us
  transfers between devices with their start and end apart: 5, of which 4 were waited for; matrix products, arithmetic and copies ran while one was open for 8% of the time, Pallas kernels for 0%

commit v1 on v0

v1 whole, which is shorter than its diff:
```python
import jax
import jax.numpy as jnp
from jax import lax
from jax.sharding import PartitionSpec as P

PHASES = 2
F32 = jnp.float32
BF16 = jnp.bfloat16


def apply_blocks(matrix, keep_mask):
    rows_blocks, cols_blocks = keep_mask.shape
    shaped = matrix.reshape(
        rows_blocks, matrix.shape[0] // rows_blocks, cols_blocks, matrix.shape[1] // cols_blocks
    )
    return (shaped * keep_mask.astype(matrix.dtype)[:, None, :, None]).reshape(matrix.shape)


def at(array, index):
    return lax.dynamic_index_in_dim(array, index, 0, keepdims=False)


def per_device(
    activations,
    upstream,
    gate_value,
    up_value,
    hidden_grad,
    gate_weight,
    up_weight,
    gate_mask,
    up_mask,
):
    n_dp, n_tensor, n_pipe = (lax.axis_size(a) for a in ("dp", "tensor", "pipe"))
    n_x = n_tensor // 4
    j = lax.axis_index("dp")
    t = lax.axis_index("tensor")
    core, x, zh = t % 2, (t // 2) % n_x, t // (2 * n_x)

    def index(zh, x, core):
        return (zh * n_x + x) * 2 + core

    places = [(a, b, c) for a in range(2) for b in range(n_x) for c in range(2)]
    swap_core = [(index(a, b, c), index(a, b, 1 - c)) for a, b, c in places]
    swap_z = [(index(a, b, c), index(1 - a, b, c)) for a, b, c in places]

    def shift_x(s):
        return [(index(a, b, c), index(a, (b + s) % n_x, c)) for a, b, c in places]

    right = [(i, (i + 1) % n_dp) for i in range(n_dp)]
    left = [(i, (i - 1) % n_dp) for i in range(n_dp)]
    half_hops = n_dp // 2

    gate_float = gate_value[0].astype(F32)
    up_float = up_value[0].astype(F32)
    hidden_float = hidden_grad[0].astype(F32)
    gate_sigmoid = jax.nn.sigmoid(gate_float)
    up_delta = (hidden_float * gate_float * gate_sigmoid).astype(BF16)
    gate_delta = (
        hidden_float * up_float * gate_sigmoid * (1.0 + gate_float * (1.0 - gate_sigmoid))
    ).astype(BF16)
    tokens, hidden = gate_delta.shape
    width = activations.shape[2]
    rows = tokens // (2 * PHASES)
    delta = jnp.concatenate([gate_delta, up_delta], axis=1)
    delta = delta.reshape(2, PHASES, rows, 2 * hidden)

    hops = []
    for p in range(PHASES):
        own = delta[:, p].reshape(2 * rows, 2 * hidden)
        steps = [own]
        going_right = going_left = own
        for h in range(1, half_hops):
            going_right = lax.ppermute(going_right, "dp", right)
            going_left = lax.ppermute(going_left, "dp", left)
            steps.append(jnp.concatenate([going_right, going_left], axis=0))
        last_right = lax.ppermute(going_right[:rows], "dp", right)
        last_left = lax.ppermute(going_left[rows:], "dp", left)
        steps.append(jnp.concatenate([last_right, last_left], axis=0))
        hops.append(steps)

    mine = activations[0]
    pair = jnp.stack([mine, lax.ppermute(mine, "tensor", swap_z)])
    around = [pair] + [lax.ppermute(pair, "tensor", shift_x(s)) for s in range(1, n_x)]
    same_core = jnp.stack(around)
    other_core = lax.ppermute(same_core, "tensor", swap_core)
    first = jnp.where(core == 0, same_core, other_core)
    second = jnp.where(core == 0, other_core, same_core)
    stored = jnp.stack([first, second], axis=2)
    stored = stored.reshape(n_x * 2, 2, PHASES, rows, width)

    def stream_of(block):
        block_x, block_z = block % n_x, block // n_x
        place = ((x - block_x) % n_x) * 2 + (block_z + zh) % 2
        return at(stored, place)

    kept = jnp.concatenate(
        [apply_blocks(gate_weight[0], gate_mask[0]), apply_blocks(up_weight[0], up_mask[0])], axis=1
    )
    over_tokens = (((0,), (0,)), ((), ()))
    over_hidden = (((1,), (1,)), ((), ()))

    order = [0]
    for h in range(1, half_hops):
        order += [n_dp - h, h]
    order.append(half_hops)
    slot = [order.index(r) for r in range(n_dp)]

    own_rows = []
    for p in range(PHASES):
        summed = []
        for group in (hops[p][: half_hops - 1], hops[p][half_hops - 1 :]):
            parts = [
                lax.dot_general(step, kept, over_hidden, preferred_element_type=F32)
                for step in group
            ]
            part = jnp.concatenate(parts, axis=0).reshape(-1, 2, rows, width)
            here = jnp.where(core == 0, part[:, 0], part[:, 1])
            there = jnp.where(core == 0, part[:, 1], part[:, 0]).astype(BF16)
            there = lax.ppermute(there, "tensor", swap_core)
            summed.append(here + there.astype(F32))
        summed = jnp.concatenate(summed, axis=0)
        slots = jnp.array(slot, jnp.int32)

        def for_chip(chip_z, chip_x):
            return at(summed, slots[(chip_z * n_x + chip_x - j) % n_dp])

        total = jnp.stack([for_chip(a, x) for a in range(2)])
        for s in range(1, n_x):
            sent = jnp.stack([for_chip(a, (x + s) % n_x) for a in range(2)]).astype(BF16)
            total = total + lax.ppermute(sent, "tensor", shift_x(s)).astype(F32)
        away = lax.ppermute(at(total, 1 - zh).astype(BF16), "tensor", swap_z)
        own_rows.append(at(total, zh) + away.astype(F32))
    branch = jnp.concatenate(own_rows, axis=0)
    section_grad = (upstream[0].astype(F32) + branch).astype(BF16)
    handed = lax.ppermute(section_grad, "pipe", [(i, i - 1) for i in range(1, n_pipe)])

    acc = None
    for h in range(half_hops + 1):
        ids = [0] if h == 0 else [n_dp - h, h] if h < half_hops else [half_hops]
        streams = [stream_of((j + r) % n_dp) for r in ids]
        lhs = jnp.concatenate(
            [s[:, p].reshape(2 * rows, width) for p in range(PHASES) for s in streams], axis=0
        )
        rhs = jnp.concatenate([hops[p][h] for p in range(PHASES)], axis=0)
        term = lax.dot_general(lhs, rhs, over_tokens, preferred_element_type=F32)
        acc = term if acc is None else acc + term
    gate_gradient = apply_blocks(acc[:, :hidden], gate_mask[0]).astype(BF16)[None]
    up_gradient = apply_blocks(acc[:, hidden:], up_mask[0]).astype(BF16)[None]
    return (gate_gradient, up_gradient, handed[None])


def solution(mesh):
    return jax.shard_map(
        per_device,
        mesh=mesh,
        in_specs=(
            P("pipe", "tensor", "dp"),
            P("pipe", "tensor", "dp"),
            P("pipe", "dp", "tensor"),
            P("pipe", "dp", "tensor"),
            P("pipe", "dp", "tensor"),
            P("pipe", "dp", "tensor"),
            P("pipe", "dp", "tensor"),
            P("pipe", "dp", "tensor"),
            P("pipe", "dp", "tensor"),
        ),
        out_specs=(P("pipe", "dp", "tensor"), P("pipe", "dp", "tensor"), P("pipe", "tensor", "dp")),
        check_vma=False,
    )
```

time: 297 us -> 190 us (0.64)
  waiting for transfers between devices: 252 us -> 15.2 us
  starting transfers between devices: 1.45 us -> 114 us
  other arithmetic: 4.23 us -> 12.2 us
  local copies, waits for them, and re-layouts: 5.86 us -> 12.9 us
  between operations: 13.9 us -> 18.4 us
  matrix products: 19.2 us -> 15.5 us
    all_gather x3 -> x0, waiting for transfers between devices: 149 us -> none  [the longest x1 60.2 us: per_device(): gathered = lax.all_gather(activations, 'tensor', axis=1, tiled=True)[0]]
    ppermute x1 -> x34, starting transfers between devices: 1.29 us -> 114 us  [the longest x6 28.7 us: per_device(): going_left = lax.ppermute(going_left, 'dp', left)]
    reduce_scatter x1 -> x0, waiting for transfers between devices: 101 us -> none  [per_device(): lax.psum_scatter(branch, 'tensor', scatter_dimension=0, tiled=True)]
    ppermute x1 -> x34, waiting for transfers between devices: 0.01 us -> 15.2 us  [the longest x2 5.82 us: per_device(): away = lax.ppermute(at(total, 1 - zh).astype(BF16), 'tensor', swap_z)]
    dot_general x4 -> x15, matrix products: 19.2 us -> 15.5 us  [the longest x10 9 us: per_device(): lax.dot_general(step, kept, over_hidden, preferred_element_type=F32)]
    mul x4 -> x6, local copies, waits for them, and re-layouts: 1.21 us -> 4.62 us  [apply_blocks(): shaped * keep_mask.astype(matrix.dtype)[:, None, :, None]]
    unnamed x13 -> x75, local copies, waits for them, and re-layouts: 4.25 us -> 6.3 us
  transfers between devices with their start and end apart: 5 -> 34, of which waited for: 4 -> 5; matrix products, arithmetic and copies ran while one was open for 8% -> 18% of each run, Pallas kernels for 0% -> 0%
where the time goes in v1:
time: 190 us; the launch traced here: 188 us
  starting transfers between devices  114 us (60%)
  between operations  18.4 us (10%)
  matrix products  15.5 us (8%)
  waiting for transfers between devices  15.2 us (8%)
  local copies, waits for them, and re-layouts  12.9 us (7%)
  other arithmetic  12.2 us (6%)
    ppermute x6, starting transfers between devices, per_device(): going_left = lax.ppermute(going_left, 'dp', left)  28.7 us
    ppermute x6, starting transfers between devices, per_device(): total = total + lax.ppermute(sent, 'tensor', shift_x(s)).astype(F32)  20.2 us
    ppermute x6, starting transfers between devices, per_device(): going_right = lax.ppermute(going_right, 'dp', right)  12.7 us
    ppermute x1, starting transfers between devices, per_device(): pair = jnp.stack([mine, lax.ppermute(mine, 'tensor', swap_z)])  10.9 us
    ppermute x2, starting transfers between devices, per_device(): last_left = lax.ppermute(going_left[rows:], 'dp', left)  10.4 us
    dot_general x10, matrix products, per_device(): lax.dot_general(step, kept, over_hidden, preferred_element_type=F32)  9 us
    ppermute x3, starting transfers between devices, per_device(): lax.ppermute(pair, 'tensor', shift_x(s))  8.77 us
    ppermute x4, starting transfers between devices, per_device(): there = lax.ppermute(there, 'tensor', swap_core)  8.63 us
  transfers between devices with their start and end apart: 34, of which 5 were waited for; matrix products, arithmetic and copies ran while one was open for 18% of the time, Pallas kernels for 0%

profile of v1, /device:TPU:6, one launch (start us, length us, event | category | flops | bytes accessed | tf_op | source)
XLA Modules:
  0.0 188.0 jit_solution(16287202354625372310)
XLA Ops:
  0.7 1.6 fusion.29
  2.4 5.4 %collective-permute-start.6 = (bf16[96,1792]{1,0:T(8,128)(2,1)S(1)}, bf16[96,1792]{1,0:T(8,128)(2,1)S(1)}, u32[]{:S(2)}, u32[]{:S(2)}) collective-permute-start(bf16[96,1792]{1,0:T(8,128)(2,1)S(1)} %bitcast.215), channel_id=1, source_target_pairs={{0,448},{64,0},{128,64},{192,128},{256,192},{320,256},{384,320},{4... | collective-permute-start | bytes 1032200 | tf_op jit(solution)/shard_map/ppermute | solution.py:75
  7.8 1.9 %collective-permute-start.5 = (bf16[96,1792]{1,0:T(8,128)(2,1)S(1)}, bf16[96,1792]{1,0:T(8,128)(2,1)}, u32[]{:S(2)}, u32[]{:S(2)}) collective-permute-start(bf16[96,1792]{1,0:T(8,128)(2,1)S(1)} %bitcast.216), channel_id=1, source_target_pairs={{0,64},{64,128},{128,192},{192,256},{256,320},{320,384},{384,448},... | collective-permute-start | bytes 1032200 | tf_op jit(solution)/shard_map/ppermute | solution.py:74
  9.7 2.0 %collective-permute-start.7 = (bf16[96,1792]{1,0:T(8,128)(2,1)S(1)}, bf16[96,1792]{1,0:T(8,128)(2,1)}, u32[]{:S(2)}, u32[]{:S(2)}) collective-permute-start(bf16[96,1792]{1,0:T(8,128)(2,1)S(1)} %bitcast.219), channel_id=1, source_target_pairs={{0,64},{64,128},{128,192},{192,256},{256,320},{320,384},{384,448},... | collective-permute-start | bytes 1032200 | tf_op jit(solution)/shard_map/ppermute | solution.py:74
  11.7 5.0 %collective-permute-start.8 = (bf16[96,1792]{1,0:T(8,128)(2,1)S(1)}, bf16[96,1792]{1,0:T(8,128)(2,1)}, u32[]{:S(2)}, u32[]{:S(2)}) collective-permute-start(bf16[96,1792]{1,0:T(8,128)(2,1)S(1)} %bitcast.220), channel_id=1, source_target_pairs={{0,448},{64,0},{128,64},{192,128},{256,192},{320,256},{384,320},{4... | collective-permute-start | bytes 1032200 | tf_op jit(solution)/shard_map/ppermute | solution.py:75
  16.8 10.9 %collective-permute-start = (bf16[96,512]{1,0:T(8,128)(2,1)S(1)}, bf16[96,512]{1,0:T(8,128)(2,1)S(1)}, u32[]{:S(2)}, u32[]{:S(2)}) collective-permute-start(bf16[96,512]{1,0:T(8,128)(2,1)S(1)} %bitcast.240), channel_id=1, source_target_pairs={{0,8},{1,9},{2,10},{3,11},{4,12},{5,13},{6,14},{7,15},{8,0},{9,1},... | collective-permute-start | bytes 294920 | tf_op jit(solution)/shard_map/ppermute | solution.py:83
  29.6 1.5 copy.28
  34.5 3.9 %collective-permute-start.10 = (bf16[96,1792]{1,0:T(8,128)(2,1)S(1)}, bf16[96,1792]{1,0:T(8,128)(2,1)S(1)}, u32[]{:S(2)}, u32[]{:S(2)}) collective-permute-start(bf16[96,1792]{1,0:T(8,128)(2,1)S(1)} %collective-permute-done.6), channel_id=1, source_target_pairs={{0,448},{64,0},{128,64},{192,128},{256,192},{320,256},{384,320},{4... | collective-permute-start | bytes 1032200 | tf_op jit(solution)/shard_map/ppermute | solution.py:75
  38.4 1.9 %collective-permute-start.9 = (bf16[96,1792]{1,0:T(8,128)(2,1)}, bf16[96,1792]{1,0:T(8,128)(2,1)S(1)}, u32[]{:S(2)}, u32[]{:S(2)}) collective-permute-start(bf16[96,1792]{1,0:T(8,128)(2,1)} %collective-permute-done.5), channel_id=1, source_target_pairs={{0,64},{64,128},{128,192},{192,256},{256,320},{320,384},{384,448},... | collective-permute-start | bytes 1032200 | tf_op jit(solution)/shard_map/ppermute | solution.py:74
  40.4 2.5 %collective-permute-start.1 = (bf16[2,96,512]{2,1,0:T(8,128)(2,1)S(1)}, bf16[2,96,512]{2,1,0:T(8,128)(2,1)S(1)}, u32[]{:S(2)}, u32[]{:S(2)}) collective-permute-start(bf16[2,96,512]{2,1,0:T(8,128)(2,1)S(1)} %get-tuple-element.52), channel_id=1, source_target_pairs={{0,2},{1,3},{2,4},{3,5},{4,6},{5,7},{6,0},{7,1},{8,10},{9,11},{10,... | collective-permute-start | bytes 589832 | tf_op jit(solution)/shard_map/ppermute | solution.py:84
  42.9 2.1 %fusion.48 = f32[192,512]{1,0:T(8,128)S(1)} fusion(bf16[96,1792]{1,0:T(8,128)(2,1)S(1)} %collective-permute-done.6, bf16[96,1792]{1,0:T(8,128)(2,1)} %collective-permute-done.5, bf16[512,896]{0,1:T(8,128)(2,1)} %copy-done.7, bf16[512,896]{0,1:T(8,128)(2,1)} %copy-done.10), kind=kOutput, calls=%fused_computation.115 | convolution fusion | flops 357367808 | bytes 2916352 | tf_op jit(solution)/shard_map/dot_general | solution.py:114
  45.0 4.3 %collective-permute-start.2 = (bf16[2,96,512]{2,1,0:T(8,128)(2,1)S(1)}, bf16[2,96,512]{2,1,0:T(8,128)(2,1)S(1)}, u32[]{:S(2)}, u32[]{:S(2)}) collective-permute-start(bf16[2,96,512]{2,1,0:T(8,128)(2,1)S(1)} %get-tuple-element.52), channel_id=1, source_target_pairs={{0,4},{1,5},{2,6},{3,7},{4,0},{5,1},{6,2},{7,3},{8,12},{9,13},{10,... | collective-permute-start | bytes 589832 | tf_op jit(solution)/shard_map/ppermute | solution.py:84
  49.4 1.9 %collective-permute-start.3 = (bf16[2,96,512]{2,1,0:T(8,128)(2,1)S(1)}, bf16[2,96,512]{2,1,0:T(8,128)(2,1)S(1)}, u32[]{:S(2)}, u32[]{:S(2)}) collective-permute-start(bf16[2,96,512]{2,1,0:T(8,128)(2,1)S(1)} %get-tuple-element.52), channel_id=1, source_target_pairs={{0,6},{1,7},{2,0},{3,1},{4,2},{5,3},{6,4},{7,5},{8,14},{9,15},{10,... | collective-permute-start | bytes 589832 | tf_op jit(solution)/shard_map/ppermute | solution.py:84
  51.3 1.6 fusion.60
  53.0 2.1 %collective-permute-start.11 = (bf16[96,1792]{1,0:T(8,128)(2,1)}, bf16[96,1792]{1,0:T(8,128)(2,1)S(1)}, u32[]{:S(2)}, u32[]{:S(2)}) collective-permute-start(bf16[96,1792]{1,0:T(8,128)(2,1)} %collective-permute-done.7), channel_id=1, source_target_pairs={{0,64},{64,128},{128,192},{192,256},{256,320},{320,384},{384,448},... | collective-permute-start | bytes 1032200 | tf_op jit(solution)/shard_map/ppermute | solution.py:74
  55.0 5.1 %collective-permute-start.12 = (bf16[96,1792]{1,0:T(8,128)(2,1)}, bf16[96,1792]{1,0:T(8,128)(2,1)S(1)}, u32[]{:S(2)}, u32[]{:S(2)}) collective-permute-start(bf16[96,1792]{1,0:T(8,128)(2,1)} %collective-permute-done.8), channel_id=1, source_target_pairs={{0,448},{64,0},{128,64},{192,128},{256,192},{320,256},{384,320},{4... | collective-permute-start | bytes 1032200 | tf_op jit(solution)/shard_map/ppermute | solution.py:75
  61.6 2.4 %collective-permute-done.11 = bf16[96,1792]{1,0:T(8,128)(2,1)S(1)} collective-permute-done((bf16[96,1792]{1,0:T(8,128)(2,1)}, bf16[96,1792]{1,0:T(8,128)(2,1)S(1)}, u32[]{:S(2)}, u32[]{:S(2)}) %collective-permute-start.11) | collective-permute-done | bytes 344096 | tf_op jit(solution)/shard_map/ppermute | solution.py:74
  64.0 1.9 %collective-permute-start.21 = (bf16[5,48,512]{2,1,0:T(8,128)(2,1)}, bf16[5,48,512]{2,1,0:T(8,128)(2,1)}, u32[]{:S(2)}, u32[]{:S(2)}) collective-permute-start(bf16[5,48,512]{2,1,0:T(8,128)(2,1)} %fusion.102), channel_id=1, source_target_pairs={{0,1},{1,0},{2,3},{3,2},{4,5},{5,4},{6,7},{7,6},{8,9},{9,8},{10,11... | collective-permute-start | bytes 737288 | tf_op jit(solution)/shard_map/ppermute | solution.py:120
  68.4 2.4 %collective-permute-start.27 = (bf16[5,48,512]{2,1,0:T(8,128)(2,1)}, bf16[5,48,512]{2,1,0:T(8,128)(2,1)}, u32[]{:S(2)}, u32[]{:S(2)}) collective-permute-start(bf16[5,48,512]{2,1,0:T(8,128)(2,1)} %fusion.103), channel_id=1, source_target_pairs={{0,1},{1,0},{2,3},{3,2},{4,5},{5,4},{6,7},{7,6},{8,9},{9,8},{10,11... | collective-permute-start | bytes 737288 | tf_op jit(solution)/shard_map/ppermute | solution.py:120
  83.2 1.9 %collective-permute-start.4 = (bf16[4,2,96,512]{3,2,1,0:T(8,128)(2,1)}, bf16[4,2,96,512]{3,2,1,0:T(8,128)(2,1)}, u32[]{:S(2)}, u32[]{:S(2)}) collective-permute-start(bf16[4,2,96,512]{3,2,1,0:T(8,128)(2,1)} %pad_maximum_fusion.3), channel_id=1, source_target_pairs={{0,1},{1,0},{2,3},{3,2},{4,5},{5,4},{6,7},{7,6},{8,9},{9,8},{10,11... | collective-permute-start | bytes 2359304 | tf_op jit(solution)/shard_map/ppermute | solution.py:86
  86.3 1.7 copy.23
  89.3 1.7 copy.25
  96.3 2.9 %collective-permute-start.13 = (bf16[96,1792]{1,0:T(8,128)(2,1)}, bf16[96,1792]{1,0:T(8,128)(2,1)S(1)}, u32[]{:S(2)}, u32[]{:S(2)}) collective-permute-start(bf16[96,1792]{1,0:T(8,128)(2,1)} %copy-done.29), channel_id=1, source_target_pairs={{0,64},{64,128},{128,192},{192,256},{256,320},{320,384},{384,448},... | collective-permute-start | bytes 1032200 | tf_op jit(solution)/shard_map/ppermute | solution.py:74
  99.2 4.2 %collective-permute-start.14 = (bf16[96,1792]{1,0:T(8,128)(2,1)}, bf16[96,1792]{1,0:T(8,128)(2,1)S(1)}, u32[]{:S(2)}, u32[]{:S(2)}) collective-permute-start(bf16[96,1792]{1,0:T(8,128)(2,1)} %copy-done.27), channel_id=1, source_target_pairs={{0,448},{64,0},{128,64},{192,128},{256,192},{320,256},{384,320},{4... | collective-permute-start | bytes 1032200 | tf_op jit(solution)/shard_map/ppermute | solution.py:75
  103.3 1.9 %collective-permute-start.15 = (bf16[96,1792]{1,0:T(8,128)(2,1)}, bf16[96,1792]{1,0:T(8,128)(2,1)S(1)}, u32[]{:S(2)}, u32[]{:S(2)}) collective-permute-start(bf16[96,1792]{1,0:T(8,128)(2,1)} %copy-done.31), channel_id=1, source_target_pairs={{0,64},{64,128},{128,192},{192,256},{256,320},{320,384},{384,448},... | collective-permute-start | bytes 1032200 | tf_op jit(solution)/shard_map/ppermute | solution.py:74
  105.3 5.1 %collective-permute-start.16 = (bf16[96,1792]{1,0:T(8,128)(2,1)}, bf16[96,1792]{1,0:T(8,128)(2,1)S(1)}, u32[]{:S(2)}, u32[]{:S(2)}) collective-permute-start(bf16[96,1792]{1,0:T(8,128)(2,1)} %copy-done.33), channel_id=1, source_target_pairs={{0,448},{64,0},{128,64},{192,128},{256,192},{320,256},{384,320},{4... | collective-permute-start | bytes 1032200 | tf_op jit(solution)/shard_map/ppermute | solution.py:75
  112.7 1.9 %collective-permute-start.17 = (bf16[48,1792]{1,0:T(8,128)(2,1)S(1)}, bf16[48,1792]{1,0:T(8,128)(2,1)S(1)}, u32[]{:S(2)}, u32[]{:S(2)}) collective-permute-start(bf16[48,1792]{1,0:T(8,128)(2,1)S(1)} %slice.154), channel_id=1, source_target_pairs={{0,64},{64,128},{128,192},{192,256},{256,320},{320,384},{384,448},... | collective-permute-start | bytes 516104 | tf_op jit(solution)/shard_map/ppermute | solution.py:77
  114.7 5.1 %collective-permute-start.18 = (bf16[48,1792]{1,0:T(8,128)(2,1)S(1)}, bf16[48,1792]{1,0:T(8,128)(2,1)S(1)}, u32[]{:S(2)}, u32[]{:S(2)}) collective-permute-start(bf16[48,1792]{1,0:T(8,128)(2,1)S(1)} %slice.155), channel_id=1, source_target_pairs={{0,448},{64,0},{128,64},{192,128},{256,192},{320,256},{384,320},{4... | collective-permute-start | bytes 516104 | tf_op jit(solution)/shard_map/ppermute | solution.py:78
  119.9 1.9 %collective-permute-start.19 = (bf16[48,1792]{1,0:T(8,128)(2,1)S(1)}, bf16[48,1792]{1,0:T(8,128)(2,1)S(1)}, u32[]{:S(2)}, u32[]{:S(2)}) collective-permute-start(bf16[48,1792]{1,0:T(8,128)(2,1)S(1)} %slice.156), channel_id=1, source_target_pairs={{0,64},{64,128},{128,192},{192,256},{256,320},{320,384},{384,448},... | collective-permute-start | bytes 516104 | tf_op jit(solution)/shard_map/ppermute | solution.py:77
  121.8 5.3 %collective-permute-start.20 = (bf16[48,1792]{1,0:T(8,128)(2,1)S(1)}, bf16[48,1792]{1,0:T(8,128)(2,1)S(1)}, u32[]{:S(2)}, u32[]{:S(2)}) collective-permute-start(bf16[48,1792]{1,0:T(8,128)(2,1)S(1)} %slice.157), channel_id=1, source_target_pairs={{0,448},{64,0},{128,64},{192,128},{256,192},{320,256},{384,320},{4... | collective-permute-start | bytes 516104 | tf_op jit(solution)/shard_map/ppermute | solution.py:78
  128.7 1.3 broadcast_select_fusion.1
  132.7 2.4 %fusion.2 = f32[512,1792]{1,0:T(8,128)S(1)} fusion(bf16[96,1792]{1,0:T(8,128)(2,1)} %collective-permute-done.8, bf16[96,1792]{1,0:T(8,128)(2,1)} %collective-permute-done.7, bf16[96,1792]{1,0:T(8,128)(2,1)S(1)} %copy-done.26, bf16[96,1792]{1,0:T(8,128)(2,1)} %collective-permute-done.5, bf16[96,512]{1,0:T(8,128)(2,1)S(1)} %bitcast.245, ...), kind=kOutput, calls=%fused_computation.56 | convolution fusion | flops 711720960 | bytes 5439488 | tf_op jit(solution)/shard_map/dot_general | solution.py:146
  136.8 1.9 %collective-permute-start.22 = (bf16[3,48,512]{2,1,0:T(8,128)(2,1)S(1)}, bf16[3,48,512]{2,1,0:T(8,128)(2,1)S(1)}, u32[]{:S(2)}, u32[]{:S(2)}) collective-permute-start(bf16[3,48,512]{2,1,0:T(8,128)(2,1)S(1)} %fusion.131), channel_id=1, source_target_pairs={{0,1},{1,0},{2,3},{3,2},{4,5},{5,4},{6,7},{7,6},{8,9},{9,8},{10,11... | collective-permute-start | bytes 442376 | tf_op jit(solution)/shard_map/ppermute | solution.py:120
  139.3 2.4 %collective-permute-start.28 = (bf16[3,48,512]{2,1,0:T(8,128)(2,1)S(1)}, bf16[3,48,512]{2,1,0:T(8,128)(2,1)S(1)}, u32[]{:S(2)}, u32[]{:S(2)}) collective-permute-start(bf16[3,48,512]{2,1,0:T(8,128)(2,1)S(1)} %fusion.132), channel_id=1, source_target_pairs={{0,1},{1,0},{2,3},{3,2},{4,5},{5,4},{6,7},{7,6},{8,9},{9,8},{10,11... | collective-permute-start | bytes 442376 | tf_op jit(solution)/shard_map/ppermute | solution.py:120
  142.4 1.5 add_add_fusion
  144.6 5.1 %collective-permute-start.23 = (bf16[2,48,512]{2,1,0:T(8,128)(2,1)S(1)}, bf16[2,48,512]{2,1,0:T(8,128)(2,1)S(1)}, u32[]{:S(2)}, u32[]{:S(2)}) collective-permute-start(bf16[2,48,512]{2,1,0:T(8,128)(2,1)S(1)} %pad_maximum_fusion.8), channel_id=1, source_target_pairs={{0,2},{1,3},{2,4},{3,5},{4,6},{5,7},{6,0},{7,1},{8,10},{9,11},{10,... | collective-permute-start | bytes 294920 | tf_op jit(solution)/shard_map/ppermute | solution.py:131
  149.7 2.0 %collective-permute-start.24 = (bf16[2,48,512]{2,1,0:T(8,128)(2,1)S(1)}, bf16[2,48,512]{2,1,0:T(8,128)(2,1)S(1)}, u32[]{:S(2)}, u32[]{:S(2)}) collective-permute-start(bf16[2,48,512]{2,1,0:T(8,128)(2,1)S(1)} %pad_maximum_fusion.9), channel_id=1, source_target_pairs={{0,4},{1,5},{2,6},{3,7},{4,0},{5,1},{6,2},{7,3},{8,12},{9,13},{10,... | collective-permute-start | bytes 294920 | tf_op jit(solution)/shard_map/ppermute | solution.py:131
  151.7 3.3 %collective-permute-start.25 = (bf16[2,48,512]{2,1,0:T(8,128)(2,1)S(1)}, bf16[2,48,512]{2,1,0:T(8,128)(2,1)S(1)}, u32[]{:S(2)}, u32[]{:S(2)}) collective-permute-start(bf16[2,48,512]{2,1,0:T(8,128)(2,1)S(1)} %pad_maximum_fusion.10), channel_id=1, source_target_pairs={{0,6},{1,7},{2,0},{3,1},{4,2},{5,3},{6,4},{7,5},{8,14},{9,15},{10,... | collective-permute-start | bytes 294920 | tf_op jit(solution)/shard_map/ppermute | solution.py:131
  155.0 3.7 %collective-permute-start.29 = (bf16[2,48,512]{2,1,0:T(8,128)(2,1)S(1)}, bf16[2,48,512]{2,1,0:T(8,128)(2,1)S(1)}, u32[]{:S(2)}, u32[]{:S(2)}) collective-permute-start(bf16[2,48,512]{2,1,0:T(8,128)(2,1)S(1)} %pad_maximum_fusion.11), channel_id=1, source_target_pairs={{0,2},{1,3},{2,4},{3,5},{4,6},{5,7},{6,0},{7,1},{8,10},{9,11},{10,... | collective-permute-start | bytes 294920 | tf_op jit(solution)/shard_map/ppermute | solution.py:131
  158.8 4.2 %collective-permute-start.30 = (bf16[2,48,512]{2,1,0:T(8,128)(2,1)S(1)}, bf16[2,48,512]{2,1,0:T(8,128)(2,1)S(1)}, u32[]{:S(2)}, u32[]{:S(2)}) collective-permute-start(bf16[2,48,512]{2,1,0:T(8,128)(2,1)S(1)} %pad_maximum_fusion.12), channel_id=1, source_target_pairs={{0,4},{1,5},{2,6},{3,7},{4,0},{5,1},{6,2},{7,3},{8,12},{9,13},{10,... | collective-permute-start | bytes 294920 | tf_op jit(solution)/shard_map/ppermute | solution.py:131
  163.0 1.9 %collective-permute-start.31 = (bf16[2,48,512]{2,1,0:T(8,128)(2,1)S(1)}, bf16[2,48,512]{2,1,0:T(8,128)(2,1)S(1)}, u32[]{:S(2)}, u32[]{:S(2)}) collective-permute-start(bf16[2,48,512]{2,1,0:T(8,128)(2,1)S(1)} %pad_maximum_fusion.13), channel_id=1, source_target_pairs={{0,6},{1,7},{2,0},{3,1},{4,2},{5,3},{6,4},{7,5},{8,14},{9,15},{10,... | collective-permute-start | bytes 294920 | tf_op jit(solution)/shard_map/ppermute | solution.py:131
  165.0 2.2 %collective-permute-start.26 = (bf16[48,512]{1,0:T(8,128)(2,1)S(1)}, bf16[48,512]{1,0:T(8,128)(2,1)S(1)}, u32[]{:S(2)}, u32[]{:S(2)}) collective-permute-start(bf16[48,512]{1,0:T(8,128)(2,1)S(1)} %fusion.161), channel_id=1, source_target_pairs={{0,8},{1,9},{2,10},{3,11},{4,12},{5,13},{6,14},{7,15},{8,0},{9,1},... | collective-permute-start | bytes 147464 | tf_op jit(solution)/shard_map/ppermute | solution.py:132
  167.3 3.5 %collective-permute-done.31 = bf16[2,48,512]{2,1,0:T(8,128)(2,1)S(1)} collective-permute-done((bf16[2,48,512]{2,1,0:T(8,128)(2,1)S(1)}, bf16[2,48,512]{2,1,0:T(8,128)(2,1)S(1)}, u32[]{:S(2)}, u32[]{:S(2)}) %collective-permute-start.31) | collective-permute-done | bytes 98336 | tf_op jit(solution)/shard_map/ppermute | solution.py:131
  170.8 4.1 %collective-permute-start.32 = (bf16[48,512]{1,0:T(8,128)(2,1)S(1)}, bf16[48,512]{1,0:T(8,128)(2,1)S(1)}, u32[]{:S(2)}, u32[]{:S(2)}) collective-permute-start(bf16[48,512]{1,0:T(8,128)(2,1)S(1)} %fusion.162), channel_id=1, source_target_pairs={{0,8},{1,9},{2,10},{3,11},{4,12},{5,13},{6,14},{7,15},{8,0},{9,1},... | collective-permute-start | bytes 147464 | tf_op jit(solution)/shard_map/ppermute | solution.py:132
  175.5 5.3 %collective-permute-done.32 = bf16[48,512]{1,0:T(8,128)(2,1)S(1)} collective-permute-done((bf16[48,512]{1,0:T(8,128)(2,1)S(1)}, bf16[48,512]{1,0:T(8,128)(2,1)S(1)}, u32[]{:S(2)}, u32[]{:S(2)}) %collective-permute-start.32) | collective-permute-done | bytes 49184 | tf_op jit(solution)/shard_map/ppermute | solution.py:132
  180.8 1.3 collective-permute-start.33
  182.1 1.8 fusion.26
  183.9 3.4 %collective-permute-done.33 = bf16[96,512]{1,0:T(8,128)(2,1)S(1)} collective-permute-done((bf16[96,512]{1,0:T(8,128)(2,1)S(1)}, bf16[96,512]{1,0:T(8,128)(2,1)S(1)}, u32[]{:S(2)}, u32[]{:S(2)}) %collective-permute-start.33) | collective-permute-done | bytes 98336 | tf_op jit(solution)/shard_map/ppermute | solution.py:136
  (169 shorter events, 24.0 us)
Async XLA Ops:
  0.6 16.1 %copy-start.19 = (bf16[1,96,512]{2,1,0:T(8,128)(2,1)S(1)}, bf16[1,96,512]{2,1,0:T(8,128)(2,1)}, u32[]{:S(2)}) copy-start(bf16[1,96,512]{2,1,0:T(8,128)(2,1)} %param.11) | copy-start | bytes 294916
  0.6 27.1 %copy-start.23 = (s32[1,4,7]{2,1,0:T(4,128)S(1)}, s32[1,4,7]{2,1,0:T(4,128)}, u32[]{:S(2)}) copy-start(s32[1,4,7]{2,1,0:T(4,128)} %param.19) | copy-start | bytes 340
  0.7 27.7 %copy-start.24 = (s32[1,4,7]{2,1,0:T(4,128)S(1)}, s32[1,4,7]{2,1,0:T(4,128)}, u32[]{:S(2)}) copy-start(s32[1,4,7]{2,1,0:T(4,128)} %param.18) | copy-start | bytes 340
  0.7 28.4 %copy-start.6 = (bf16[1,512,896]{2,1,0:T(8,128)(2,1)S(1)}, bf16[1,512,896]{2,1,0:T(8,128)(2,1)}, u32[]{:S(2)}) copy-start(bf16[1,512,896]{2,1,0:T(8,128)(2,1)} %param.16) | copy-start | bytes 2752516
  2.4 30.9 %copy-start.4 = (bf16[2,1,48,1792]{3,2,1,0:T(8,128)(2,1)}, bf16[2,1,48,1792]{3,2,1,0:T(8,128)(2,1)S(1)}, u32[]{:S(2)}) copy-start(bf16[2,1,48,1792]{3,2,1,0:T(8,128)(2,1)S(1)} %get-tuple-element.32) | copy-start | bytes 1032196
  2.4 32.1 %collective-permute-start.6 = (bf16[96,1792]{1,0:T(8,128)(2,1)S(1)}, bf16[96,1792]{1,0:T(8,128)(2,1)S(1)}, u32[]{:S(2)}, u32[]{:S(2)}) collective-permute-start(bf16[96,1792]{1,0:T(8,128)(2,1)S(1)} %bitcast.215), channel_id=1, source_target_pairs={{0,448},{64,0},{128,64},{192,128},{256,192},{320,256},{384,320},{4... | collective-permute-start | bytes 1032200 | tf_op jit(solution)/shard_map/ppermute | solution.py:75
  7.8 30.6 %collective-permute-start.5 = (bf16[96,1792]{1,0:T(8,128)(2,1)S(1)}, bf16[96,1792]{1,0:T(8,128)(2,1)}, u32[]{:S(2)}, u32[]{:S(2)}) collective-permute-start(bf16[96,1792]{1,0:T(8,128)(2,1)S(1)} %bitcast.216), channel_id=1, source_target_pairs={{0,64},{64,128},{128,192},{192,256},{256,320},{320,384},{384,448},... | collective-permute-start | bytes 1032200 | tf_op jit(solution)/shard_map/ppermute | solution.py:74
  9.7 35.3 %collective-permute-start.7 = (bf16[96,1792]{1,0:T(8,128)(2,1)S(1)}, bf16[96,1792]{1,0:T(8,128)(2,1)}, u32[]{:S(2)}, u32[]{:S(2)}) collective-permute-start(bf16[96,1792]{1,0:T(8,128)(2,1)S(1)} %bitcast.219), channel_id=1, source_target_pairs={{0,64},{64,128},{128,192},{192,256},{256,320},{320,384},{384,448},... | collective-permute-start | bytes 1032200 | tf_op jit(solution)/shard_map/ppermute | solution.py:74
  11.7 37.6 %collective-permute-start.8 = (bf16[96,1792]{1,0:T(8,128)(2,1)S(1)}, bf16[96,1792]{1,0:T(8,128)(2,1)}, u32[]{:S(2)}, u32[]{:S(2)}) collective-permute-start(bf16[96,1792]{1,0:T(8,128)(2,1)S(1)} %bitcast.220), channel_id=1, source_target_pairs={{0,448},{64,0},{128,64},{192,128},{256,192},{320,256},{384,320},{4... | collective-permute-start | bytes 1032200 | tf_op jit(solution)/shard_map/ppermute | solution.py:75
  16.8 23.5 %collective-permute-start = (bf16[96,512]{1,0:T(8,128)(2,1)S(1)}, bf16[96,512]{1,0:T(8,128)(2,1)S(1)}, u32[]{:S(2)}, u32[]{:S(2)}) collective-permute-start(bf16[96,512]{1,0:T(8,128)(2,1)S(1)} %bitcast.240), channel_id=1, source_target_pairs={{0,8},{1,9},{2,10},{3,11},{4,12},{5,13},{6,14},{7,15},{8,0},{9,1},... | collective-permute-start | bytes 294920 | tf_op jit(solution)/shard_map/ppermute | solution.py:83
  34.5 18.5 %collective-permute-start.10 = (bf16[96,1792]{1,0:T(8,128)(2,1)S(1)}, bf16[96,1792]{1,0:T(8,128)(2,1)S(1)}, u32[]{:S(2)}, u32[]{:S(2)}) collective-permute-start(bf16[96,1792]{1,0:T(8,128)(2,1)S(1)} %collective-permute-done.6), channel_id=1, source_target_pairs={{0,448},{64,0},{128,64},{192,128},{256,192},{320,256},{384,320},{4... | collective-permute-start | bytes 1032200 | tf_op jit(solution)/shard_map/ppermute | solution.py:75
  38.4 16.6 %collective-permute-start.9 = (bf16[96,1792]{1,0:T(8,128)(2,1)}, bf16[96,1792]{1,0:T(8,128)(2,1)S(1)}, u32[]{:S(2)}, u32[]{:S(2)}) collective-permute-start(bf16[96,1792]{1,0:T(8,128)(2,1)} %collective-permute-done.5), channel_id=1, source_target_pairs={{0,64},{64,128},{128,192},{192,256},{256,320},{320,384},{384,448},... | collective-permute-start | bytes 1032200 | tf_op jit(solution)/shard_map/ppermute | solution.py:74
  40.4 10.9 %copy-start.8 = (bf16[512,896]{0,1:T(8,128)(2,1)S(1)}, bf16[512,896]{0,1:T(8,128)(2,1)}, u32[]{:S(2)}) copy-start(bf16[512,896]{0,1:T(8,128)(2,1)} %copy-done.7) | copy-start | bytes 2752516
  40.4 10.9 %copy-start.11 = (bf16[512,896]{0,1:T(8,128)(2,1)S(1)}, bf16[512,896]{0,1:T(8,128)(2,1)}, u32[]{:S(2)}) copy-start(bf16[512,896]{0,1:T(8,128)(2,1)} %copy-done.10) | copy-start | bytes 2752516
  40.4 41.8 %collective-permute-start.1 = (bf16[2,96,512]{2,1,0:T(8,128)(2,1)S(1)}, bf16[2,96,512]{2,1,0:T(8,128)(2,1)S(1)}, u32[]{:S(2)}, u32[]{:S(2)}) collective-permute-start(bf16[2,96,512]{2,1,0:T(8,128)(2,1)S(1)} %get-tuple-element.52), channel_id=1, source_target_pairs={{0,2},{1,3},{2,4},{3,5},{4,6},{5,7},{6,0},{7,1},{8,10},{9,11},{10,... | collective-permute-start | bytes 589832 | tf_op jit(solution)/shard_map/ppermute | solution.py:84
  45.0 37.1 %collective-permute-start.2 = (bf16[2,96,512]{2,1,0:T(8,128)(2,1)S(1)}, bf16[2,96,512]{2,1,0:T(8,128)(2,1)S(1)}, u32[]{:S(2)}, u32[]{:S(2)}) collective-permute-start(bf16[2,96,512]{2,1,0:T(8,128)(2,1)S(1)} %get-tuple-element.52), channel_id=1, source_target_pairs={{0,4},{1,5},{2,6},{3,7},{4,0},{5,1},{6,2},{7,3},{8,12},{9,13},{10,... | collective-permute-start | bytes 589832 | tf_op jit(solution)/shard_map/ppermute | solution.py:84
  49.4 32.8 %collective-permute-start.3 = (bf16[2,96,512]{2,1,0:T(8,128)(2,1)S(1)}, bf16[2,96,512]{2,1,0:T(8,128)(2,1)S(1)}, u32[]{:S(2)}, u32[]{:S(2)}) collective-permute-start(bf16[2,96,512]{2,1,0:T(8,128)(2,1)S(1)} %get-tuple-element.52), channel_id=1, source_target_pairs={{0,6},{1,7},{2,0},{3,1},{4,2},{5,3},{6,4},{7,5},{8,14},{9,15},{10,... | collective-permute-start | bytes 589832 | tf_op jit(solution)/shard_map/ppermute | solution.py:84
  53.0 11.0 %collective-permute-start.11 = (bf16[96,1792]{1,0:T(8,128)(2,1)}, bf16[96,1792]{1,0:T(8,128)(2,1)S(1)}, u32[]{:S(2)}, u32[]{:S(2)}) collective-permute-start(bf16[96,1792]{1,0:T(8,128)(2,1)} %collective-permute-done.7), channel_id=1, source_target_pairs={{0,64},{64,128},{128,192},{192,256},{256,320},{320,384},{384,448},... | collective-permute-start | bytes 1032200 | tf_op jit(solution)/shard_map/ppermute | solution.py:74
  55.0 10.9 %collective-permute-start.12 = (bf16[96,1792]{1,0:T(8,128)(2,1)}, bf16[96,1792]{1,0:T(8,128)(2,1)S(1)}, u32[]{:S(2)}, u32[]{:S(2)}) collective-permute-start(bf16[96,1792]{1,0:T(8,128)(2,1)} %collective-permute-done.8), channel_id=1, source_target_pairs={{0,448},{64,0},{128,64},{192,128},{256,192},{320,256},{384,320},{4... | collective-permute-start | bytes 1032200 | tf_op jit(solution)/shard_map/ppermute | solution.py:75
  64.0 39.3 %collective-permute-start.21 = (bf16[5,48,512]{2,1,0:T(8,128)(2,1)}, bf16[5,48,512]{2,1,0:T(8,128)(2,1)}, u32[]{:S(2)}, u32[]{:S(2)}) collective-permute-start(bf16[5,48,512]{2,1,0:T(8,128)(2,1)} %fusion.102), channel_id=1, source_target_pairs={{0,1},{1,0},{2,3},{3,2},{4,5},{5,4},{6,7},{7,6},{8,9},{9,8},{10,11... | collective-permute-start | bytes 737288 | tf_op jit(solution)/shard_map/ppermute | solution.py:120
  67.7 18.0 %copy-start.22 = (f32[4,7]{1,0:T(4,128)S(1)}, f32[4,7]{1,0:T(4,128)}, u32[]{:S(2)}) copy-start(f32[4,7]{1,0:T(4,128)} %get-tuple-element.54) | copy-start | bytes 340
  68.4 36.8 %collective-permute-start.27 = (bf16[5,48,512]{2,1,0:T(8,128)(2,1)}, bf16[5,48,512]{2,1,0:T(8,128)(2,1)}, u32[]{:S(2)}, u32[]{:S(2)}) collective-permute-start(bf16[5,48,512]{2,1,0:T(8,128)(2,1)} %fusion.103), channel_id=1, source_target_pairs={{0,1},{1,0},{2,3},{3,2},{4,5},{5,4},{6,7},{7,6},{8,9},{9,8},{10,11... | collective-permute-start | bytes 737288 | tf_op jit(solution)/shard_map/ppermute | solution.py:120
  83.2 45.0 %collective-permute-start.4 = (bf16[4,2,96,512]{3,2,1,0:T(8,128)(2,1)}, bf16[4,2,96,512]{3,2,1,0:T(8,128)(2,1)}, u32[]{:S(2)}, u32[]{:S(2)}) collective-permute-start(bf16[4,2,96,512]{3,2,1,0:T(8,128)(2,1)} %pad_maximum_fusion.3), channel_id=1, source_target_pairs={{0,1},{1,0},{2,3},{3,2},{4,5},{5,4},{6,7},{7,6},{8,9},{9,8},{10,11... | collective-permute-start | bytes 2359304 | tf_op jit(solution)/shard_map/ppermute | solution.py:86
  91.0 20.5 %copy-start.3 = (f32[480,512]{1,0:T(8,128)S(1)}, f32[480,512]{1,0:T(8,128)}, u32[]{:S(2)}) copy-start(f32[480,512]{1,0:T(8,128)} %copy-done.2) | copy-start | bytes 2949124
  96.3 16.5 %collective-permute-start.13 = (bf16[96,1792]{1,0:T(8,128)(2,1)}, bf16[96,1792]{1,0:T(8,128)(2,1)S(1)}, u32[]{:S(2)}, u32[]{:S(2)}) collective-permute-start(bf16[96,1792]{1,0:T(8,128)(2,1)} %copy-done.29), channel_id=1, source_target_pairs={{0,64},{64,128},{128,192},{192,256},{256,320},{320,384},{384,448},... | collective-permute-start | bytes 1032200 | tf_op jit(solution)/shard_map/ppermute | solution.py:74
  99.2 15.5 %collective-permute-start.14 = (bf16[96,1792]{1,0:T(8,128)(2,1)}, bf16[96,1792]{1,0:T(8,128)(2,1)S(1)}, u32[]{:S(2)}, u32[]{:S(2)}) collective-permute-start(bf16[96,1792]{1,0:T(8,128)(2,1)} %copy-done.27), channel_id=1, source_target_pairs={{0,448},{64,0},{128,64},{192,128},{256,192},{320,256},{384,320},{4... | collective-permute-start | bytes 1032200 | tf_op jit(solution)/shard_map/ppermute | solution.py:75
  103.3 16.5 %collective-permute-start.15 = (bf16[96,1792]{1,0:T(8,128)(2,1)}, bf16[96,1792]{1,0:T(8,128)(2,1)S(1)}, u32[]{:S(2)}, u32[]{:S(2)}) collective-permute-start(bf16[96,1792]{1,0:T(8,128)(2,1)} %copy-done.31), channel_id=1, source_target_pairs={{0,64},{64,128},{128,192},{192,256},{256,320},{320,384},{384,448},... | collective-permute-start | bytes 1032200 | tf_op jit(solution)/shard_map/ppermute | solution.py:74
  105.3 16.5 %collective-permute-start.16 = (bf16[96,1792]{1,0:T(8,128)(2,1)}, bf16[96,1792]{1,0:T(8,128)(2,1)S(1)}, u32[]{:S(2)}, u32[]{:S(2)}) collective-permute-start(bf16[96,1792]{1,0:T(8,128)(2,1)} %copy-done.33), channel_id=1, source_target_pairs={{0,448},{64,0},{128,64},{192,128},{256,192},{320,256},{384,320},{4... | collective-permute-start | bytes 1032200 | tf_op jit(solution)/shard_map/ppermute | solution.py:75
  111.5 15.7 %copy-start.9 = (bf16[512,896]{0,1:T(8,128)(2,1)S(1)}, bf16[512,896]{0,1:T(8,128)(2,1)}, u32[]{:S(2)}) copy-start(bf16[512,896]{0,1:T(8,128)(2,1)} %copy-done.7) | copy-start | bytes 2752516
  111.5 15.7 %copy-start.12 = (bf16[512,896]{0,1:T(8,128)(2,1)S(1)}, bf16[512,896]{0,1:T(8,128)(2,1)}, u32[]{:S(2)}) copy-start(bf16[512,896]{0,1:T(8,128)(2,1)} %copy-done.10) | copy-start | bytes 2752516
  112.7 23.6 %collective-permute-start.17 = (bf16[48,1792]{1,0:T(8,128)(2,1)S(1)}, bf16[48,1792]{1,0:T(8,128)(2,1)S(1)}, u32[]{:S(2)}, u32[]{:S(2)}) collective-permute-start(bf16[48,1792]{1,0:T(8,128)(2,1)S(1)} %slice.154), channel_id=1, source_target_pairs={{0,64},{64,128},{128,192},{192,256},{256,320},{320,384},{384,448},... | collective-permute-start | bytes 516104 | tf_op jit(solution)/shard_map/ppermute | solution.py:77
  114.7 21.6 %collective-permute-start.18 = (bf16[48,1792]{1,0:T(8,128)(2,1)S(1)}, bf16[48,1792]{1,0:T(8,128)(2,1)S(1)}, u32[]{:S(2)}, u32[]{:S(2)}) collective-permute-start(bf16[48,1792]{1,0:T(8,128)(2,1)S(1)} %slice.155), channel_id=1, source_target_pairs={{0,448},{64,0},{128,64},{192,128},{256,192},{320,256},{384,320},{4... | collective-permute-start | bytes 516104 | tf_op jit(solution)/shard_map/ppermute | solution.py:78
  119.9 18.9 %collective-permute-start.19 = (bf16[48,1792]{1,0:T(8,128)(2,1)S(1)}, bf16[48,1792]{1,0:T(8,128)(2,1)S(1)}, u32[]{:S(2)}, u32[]{:S(2)}) collective-permute-start(bf16[48,1792]{1,0:T(8,128)(2,1)S(1)} %slice.156), channel_id=1, source_target_pairs={{0,64},{64,128},{128,192},{192,256},{256,320},{320,384},{384,448},... | collective-permute-start | bytes 516104 | tf_op jit(solution)/shard_map/ppermute | solution.py:77
  121.8 16.9 %collective-permute-start.20 = (bf16[48,1792]{1,0:T(8,128)(2,1)S(1)}, bf16[48,1792]{1,0:T(8,128)(2,1)S(1)}, u32[]{:S(2)}, u32[]{:S(2)}) collective-permute-start(bf16[48,1792]{1,0:T(8,128)(2,1)S(1)} %slice.157), channel_id=1, source_target_pairs={{0,448},{64,0},{128,64},{192,128},{256,192},{320,256},{384,320},{4... | collective-permute-start | bytes 516104 | tf_op jit(solution)/shard_map/ppermute | solution.py:78
  136.8 7.1 %collective-permute-start.22 = (bf16[3,48,512]{2,1,0:T(8,128)(2,1)S(1)}, bf16[3,48,512]{2,1,0:T(8,128)(2,1)S(1)}, u32[]{:S(2)}, u32[]{:S(2)}) collective-permute-start(bf16[3,48,512]{2,1,0:T(8,128)(2,1)S(1)} %fusion.131), channel_id=1, source_target_pairs={{0,1},{1,0},{2,3},{3,2},{4,5},{5,4},{6,7},{7,6},{8,9},{9,8},{10,11... | collective-permute-start | bytes 442376 | tf_op jit(solution)/shard_map/ppermute | solution.py:120
  139.3 4.9 %collective-permute-start.28 = (bf16[3,48,512]{2,1,0:T(8,128)(2,1)S(1)}, bf16[3,48,512]{2,1,0:T(8,128)(2,1)S(1)}, u32[]{:S(2)}, u32[]{:S(2)}) collective-permute-start(bf16[3,48,512]{2,1,0:T(8,128)(2,1)S(1)} %fusion.132), channel_id=1, source_target_pairs={{0,1},{1,0},{2,3},{3,2},{4,5},{5,4},{6,7},{7,6},{8,9},{9,8},{10,11... | collective-permute-start | bytes 442376 | tf_op jit(solution)/shard_map/ppermute | solution.py:120
  144.4 36.3 %copy-start.20 = (bf16[1,96,512]{2,1,0:T(8,128)(2,1)S(1)}, bf16[1,96,512]{2,1,0:T(8,128)(2,1)}, u32[]{:S(2)}) copy-start(bf16[1,96,512]{2,1,0:T(8,128)(2,1)} %param.12) | copy-start | bytes 294916
  144.5 37.6 %copy-start = (f32[512,896]{1,0:T(8,128)S(1)}, f32[512,896]{1,0:T(8,128)}, u32[]{:S(2)}) copy-start(f32[512,896]{1,0:T(8,128)} %copy.23) | copy-start | bytes 5505028
  144.5 37.6 %copy-start.1 = (f32[512,896]{1,0:T(8,128)S(1)}, f32[512,896]{1,0:T(8,128)}, u32[]{:S(2)}) copy-start(f32[512,896]{1,0:T(8,128)} %copy.25) | copy-start | bytes 5505028
  144.6 18.4 %collective-permute-start.23 = (bf16[2,48,512]{2,1,0:T(8,128)(2,1)S(1)}, bf16[2,48,512]{2,1,0:T(8,128)(2,1)S(1)}, u32[]{:S(2)}, u32[]{:S(2)}) collective-permute-start(bf16[2,48,512]{2,1,0:T(8,128)(2,1)S(1)} %pad_maximum_fusion.8), channel_id=1, source_target_pairs={{0,2},{1,3},{2,4},{3,5},{4,6},{5,7},{6,0},{7,1},{8,10},{9,11},{10,... | collective-permute-start | bytes 294920 | tf_op jit(solution)/shard_map/ppermute | solution.py:131
  149.7 15.2 %collective-permute-start.24 = (bf16[2,48,512]{2,1,0:T(8,128)(2,1)S(1)}, bf16[2,48,512]{2,1,0:T(8,128)(2,1)S(1)}, u32[]{:S(2)}, u32[]{:S(2)}) collective-permute-start(bf16[2,48,512]{2,1,0:T(8,128)(2,1)S(1)} %pad_maximum_fusion.9), channel_id=1, source_target_pairs={{0,4},{1,5},{2,6},{3,7},{4,0},{5,1},{6,2},{7,3},{8,12},{9,13},{10,... | collective-permute-start | bytes 294920 | tf_op jit(solution)/shard_map/ppermute | solution.py:131
  151.7 13.3 %collective-permute-start.25 = (bf16[2,48,512]{2,1,0:T(8,128)(2,1)S(1)}, bf16[2,48,512]{2,1,0:T(8,128)(2,1)S(1)}, u32[]{:S(2)}, u32[]{:S(2)}) collective-permute-start(bf16[2,48,512]{2,1,0:T(8,128)(2,1)S(1)} %pad_maximum_fusion.10), channel_id=1, source_target_pairs={{0,6},{1,7},{2,0},{3,1},{4,2},{5,3},{6,4},{7,5},{8,14},{9,15},{10,... | collective-permute-start | bytes 294920 | tf_op jit(solution)/shard_map/ppermute | solution.py:131
  155.0 12.2 %collective-permute-start.29 = (bf16[2,48,512]{2,1,0:T(8,128)(2,1)S(1)}, bf16[2,48,512]{2,1,0:T(8,128)(2,1)S(1)}, u32[]{:S(2)}, u32[]{:S(2)}) collective-permute-start(bf16[2,48,512]{2,1,0:T(8,128)(2,1)S(1)} %pad_maximum_fusion.11), channel_id=1, source_target_pairs={{0,2},{1,3},{2,4},{3,5},{4,6},{5,7},{6,0},{7,1},{8,10},{9,11},{10,... | collective-permute-start | bytes 294920 | tf_op jit(solution)/shard_map/ppermute | solution.py:131
  158.8 8.5 %collective-permute-start.30 = (bf16[2,48,512]{2,1,0:T(8,128)(2,1)S(1)}, bf16[2,48,512]{2,1,0:T(8,128)(2,1)S(1)}, u32[]{:S(2)}, u32[]{:S(2)}) collective-permute-start(bf16[2,48,512]{2,1,0:T(8,128)(2,1)S(1)} %pad_maximum_fusion.12), channel_id=1, source_target_pairs={{0,4},{1,5},{2,6},{3,7},{4,0},{5,1},{6,2},{7,3},{8,12},{9,13},{10,... | collective-permute-start | bytes 294920 | tf_op jit(solution)/shard_map/ppermute | solution.py:131
  163.0 7.7 %collective-permute-start.31 = (bf16[2,48,512]{2,1,0:T(8,128)(2,1)S(1)}, bf16[2,48,512]{2,1,0:T(8,128)(2,1)S(1)}, u32[]{:S(2)}, u32[]{:S(2)}) collective-permute-start(bf16[2,48,512]{2,1,0:T(8,128)(2,1)S(1)} %pad_maximum_fusion.13), channel_id=1, source_target_pairs={{0,6},{1,7},{2,0},{3,1},{4,2},{5,3},{6,4},{7,5},{8,14},{9,15},{10,... | collective-permute-start | bytes 294920 | tf_op jit(solution)/shard_map/ppermute | solution.py:131
  165.0 10.4 %collective-permute-start.26 = (bf16[48,512]{1,0:T(8,128)(2,1)S(1)}, bf16[48,512]{1,0:T(8,128)(2,1)S(1)}, u32[]{:S(2)}, u32[]{:S(2)}) collective-permute-start(bf16[48,512]{1,0:T(8,128)(2,1)S(1)} %fusion.161), channel_id=1, source_target_pairs={{0,8},{1,9},{2,10},{3,11},{4,12},{5,13},{6,14},{7,15},{8,0},{9,1},... | collective-permute-start | bytes 147464 | tf_op jit(solution)/shard_map/ppermute | solution.py:132
  170.8 9.9 %collective-permute-start.32 = (bf16[48,512]{1,0:T(8,128)(2,1)S(1)}, bf16[48,512]{1,0:T(8,128)(2,1)S(1)}, u32[]{:S(2)}, u32[]{:S(2)}) collective-permute-start(bf16[48,512]{1,0:T(8,128)(2,1)S(1)} %fusion.162), channel_id=1, source_target_pairs={{0,8},{1,9},{2,10},{3,11},{4,12},{5,13},{6,14},{7,15},{8,0},{9,1},... | collective-permute-start | bytes 147464 | tf_op jit(solution)/shard_map/ppermute | solution.py:132
  180.8 6.5 %collective-permute-start.33 = (bf16[96,512]{1,0:T(8,128)(2,1)S(1)}, bf16[96,512]{1,0:T(8,128)(2,1)S(1)}, u32[]{:S(2)}, u32[]{:S(2)}) collective-permute-start(bf16[96,512]{1,0:T(8,128)(2,1)S(1)} %fusion.122), channel_id=1, source_target_pairs={{16,0},{32,16},{48,32},{17,1},{33,17},{49,33},{18,2},{34,18},{50,3... | collective-permute-start | bytes 294920 | tf_op jit(solution)/shard_map/ppermute | solution.py:136
  (21 other events, 72.1 us)

commit v2 on v0

v2 whole, which is shorter than its diff:
```python
import jax
import jax.numpy as jnp
from jax import lax
from jax.experimental import pallas as pl
from jax.experimental.pallas import tpu as pltpu
from jax.sharding import PartitionSpec as P

F32 = jnp.float32
BF16 = jnp.bfloat16
MESH = pl.DeviceIdType.MESH
N_DP, N_X, N_PIPE = 8, 4, 4
CHIPS = 2 * N_X
HOPS = N_DP // 2
BLOCK = 128


def kernel(
    delta_ref, act_ref, up_ref, gate_w, up_w, gate_mask, up_mask,
    gate_out, up_out, handed_out,
    ring, act, act_rows, act_cols, kept, part, total,
    core_send, core_recv, x_send, x_recv, z_send, z_recv, pipe_send, pipe_recv,
    send_sem, recv_sem, local_sem,
):
    rows, hidden2 = delta_ref.shape[1:]
    hidden = hidden2 // 2
    width = act_ref.shape[1]
    j = lax.axis_index("dp")
    t = lax.axis_index("tensor")
    pipe = lax.axis_index("pipe")
    core, x, zh = t % 2, (t // 2) % N_X, t // (2 * N_X)
    chip = t // 2

    def tensor_at(z, x, c):
        return {"tensor": (z * N_X + x) * 2 + c}

    right, left = {"dp": (j + 1) % N_DP}, {"dp": (j + N_DP - 1) % N_DP}
    other_core = tensor_at(zh, x, 1 - core)
    other_z = tensor_at(1 - zh, x, core)
    along_x = [None] + [tensor_at(zh, (x + s) % N_X, core) for s in range(1, N_X)]
    before = {"pipe": (pipe + N_PIPE - 1) % N_PIPE}
    after = {"pipe": (pipe + 1) % N_PIPE}

    barrier = pltpu.get_barrier_semaphore()
    greeted = [right, left, other_core, other_z, before, after] + along_x[1:]
    for other in greeted:
        pl.semaphore_signal(barrier, inc=1, device_id=other, device_id_type=MESH)
    pl.semaphore_wait(barrier, len(greeted))

    used = [0]
    sent = []

    def copy(src, dst, target):
        k = used[0]
        used[0] += 1
        made = pltpu.make_async_remote_copy(
            src_ref=src, dst_ref=dst, send_sem=send_sem.at[k], recv_sem=recv_sem.at[k],
            device_id=target, device_id_type=MESH,
        )
        return made

    def start(made):
        made.start()
        sent.append(made)
        return made

    going = {}

    def launch(d, p, h, c):
        q = 2 * p + c
        if h == 1:
            src = delta_ref.at[q]
        else:
            src = ring.at[2 * h - 3 if d == 0 else 2 * h - 2, q]
        dst = ring.at[N_DP - 1 if h == HOPS else (2 * h - 1 if d == 0 else 2 * h), q]
        going[d, p, h, c] = start(copy(src, dst, right if d == 0 else left))

    def arrive(p, h, c):
        for d in range(2):
            going[d, p, h, c].wait_recv()
            if h < HOPS - 1:
                launch(d, p, h + 1, c)
            elif d == c:
                launch(d, p, HOPS, c)

    for c in range(2):
        for d in range(2):
            launch(d, 0, 1, c)

    act_z = start(copy(act_ref, act.at[core, chip], other_z))
    act_own = [
        start(copy(act_ref, act.at[core, chip], along_x[s])) for s in range(1, N_X)
    ]
    home = pltpu.make_async_copy(act_ref, act.at[core, chip], local_sem)
    home.start()

    ring[0] = delta_ref[...]

    def keep(k, carry):
        at = pl.multiple_of(k * BLOCK, BLOCK)
        for w, (weight, mask) in enumerate(((gate_w, gate_mask), (up_w, up_mask))):
            to = pl.multiple_of(w * hidden + k * BLOCK, BLOCK)
            for i in range(width // BLOCK):
                block = weight[i * BLOCK : (i + 1) * BLOCK, pl.ds(at, BLOCK)].astype(F32)
                block = block * mask[i, k].astype(F32)
                kept[pl.ds(to, BLOCK), i * BLOCK : (i + 1) * BLOCK] = block.T.astype(BF16)
        return carry

    lax.fori_loop(0, hidden // BLOCK, keep, 0)

    core_going = {}

    def places(h):
        return (0, 1) if h == 0 else (N_DP - 1, 1) if h == HOPS else (2 * h - 1, 2)

    def multiply(p, h):
        first, n = places(h)
        lhs = ring[first : first + n, 2 * p : 2 * p + 2].reshape(n * 2 * rows, hidden2)
        out = jnp.dot(lhs, kept[...], preferred_element_type=F32)
        part[p, first : first + n] = out.reshape(n, 2, rows, width)
        for k in range(first, first + n):
            core_send[p, k] = part[p, k, 1 - core].astype(BF16)

    def send_core(p, h):
        first, n = places(h)
        core_going[p, h] = start(
            copy(core_send.at[p, pl.ds(first, n)], core_recv.at[p, pl.ds(first, n)], other_core)
        )

    x_going, z_going, pipe_going = {}, {}, {}

    def place_of(chip_z, chip_x):
        r = (chip_z * N_X + chip_x - j + N_DP) % N_DP
        return 2 * r + (r // 4) * (15 - 4 * r)

    def reduce_core(p):
        for h in range(HOPS + 1):
            core_going[p, h].wait_recv()
        for k in range(N_DP):
            total[p, k] = part[p, k, core] + core_recv[p, k].astype(F32)
        for s in (2, 1, 3):
            for a in range(2):
                x_send[p, s - 1, a] = total[p, place_of(a, (x + s) % N_X)].astype(BF16)
        for s in (2, 1, 3):
            x_going[p, s] = start(copy(x_send.at[p, s - 1], x_recv.at[p, s - 1], along_x[s]))

    def x_sum(p, a):
        value = total[p, place_of(a, x)]
        for s in range(1, N_X):
            value = value + x_recv[p, s - 1, a].astype(F32)
        return value

    def reduce_x(p):
        for s in range(1, N_X):
            x_going[p, s].wait_recv()
        z_send[p] = x_sum(p, 1 - zh).astype(BF16)
        z_going[p] = start(copy(z_send.at[p], z_recv.at[p], other_z))

    def reduce_z(p):
        own = x_sum(p, zh)
        z_going[p].wait_recv()
        own = own + z_recv[p].astype(F32) + up_ref[p * rows : (p + 1) * rows, :].astype(F32)
        pipe_send[p] = own.astype(BF16)
        made = copy(pipe_send.at[p], pipe_recv.at[p], before)
        pipe_going[p] = made

        @pl.when(pipe > 0)
        def _():
            made.start()

    multiply(0, 0)
    send_core(0, 0)
    for h in range(1, HOPS - 1):
        for c in range(2):
            arrive(0, h, c)
        multiply(0, h)
        send_core(0, h)
        if h == 1:
            act_z.wait_recv()
            far = act.at[core, (1 - zh) * N_X + x]
            act_far = [start(copy(far, far, along_x[s])) for s in range(1, N_X)]
    arrive(0, HOPS - 1, 0)
    launch(1, 1, 1, 0)
    arrive(0, HOPS - 1, 1)
    launch(0, 1, 1, 0)
    launch(0, 1, 1, 1)
    launch(1, 1, 1, 1)
    multiply(0, HOPS - 1)
    send_core(0, HOPS - 1)
    for made in act_own + act_far:
        made.wait_recv()
    home.wait()
    act_core = start(copy(act.at[core], act.at[core], other_core))
    for d in range(2):
        going[d, 0, HOPS, d].wait_recv()
    multiply(0, HOPS)
    send_core(0, HOPS)

    multiply(1, 0)
    send_core(1, 0)
    for c in range(2):
        arrive(1, 1, c)
    reduce_core(0)
    multiply(1, 1)
    send_core(1, 1)
    for c in range(2):
        arrive(1, 2, c)
    reduce_x(0)
    multiply(1, 2)
    send_core(1, 2)
    act_core.wait_recv()
    distance = [0, 7, 1, 6, 2, 5, 3, 4]
    for k in range(N_DP):
        block = (j + distance[k]) % N_DP
        for p in range(2):
            for c in range(2):
                at = ((k * 2 + p) * 2 + c) * rows
                act_rows[at : at + rows, :] = act[c, block, p * rows : (p + 1) * rows, :]

    def turn(k, carry):
        at = pl.multiple_of(k * BLOCK, BLOCK)
        act_cols[:, pl.ds(at, BLOCK)] = act_rows[pl.ds(at, BLOCK), :].astype(F32).T.astype(BF16)
        return carry

    lax.fori_loop(0, act_rows.shape[0] // BLOCK, turn, 0)
    for c in range(2):
        arrive(1, HOPS - 1, c)
    multiply(1, HOPS - 1)
    send_core(1, HOPS - 1)
    reduce_z(0)
    for d in range(2):
        going[d, 1, HOPS, d].wait_recv()
    multiply(1, HOPS)
    send_core(1, HOPS)

    def gradient(w, at, wide, first_block):
        out, mask = ((gate_out, gate_mask), (up_out, up_mask))[w]
        rhs = ring[:, :, :, pl.ds(w * hidden + at, wide)].reshape(-1, wide)
        acc = jnp.dot(act_cols[...], rhs, preferred_element_type=F32)
        for i in range(width // BLOCK):
            for b in range(wide // BLOCK):
                block = acc[i * BLOCK : (i + 1) * BLOCK, b * BLOCK : (b + 1) * BLOCK]
                block = block * mask[i, first_block + b].astype(F32)
                out[i * BLOCK : (i + 1) * BLOCK, pl.ds(at + b * BLOCK, BLOCK)] = block.astype(BF16)

    def gradients(w):
        wide = 2 * BLOCK
        whole = hidden // wide

        def step(k, carry):
            gradient(w, pl.multiple_of(k * wide, wide), wide, 2 * k)
            return carry

        lax.fori_loop(0, whole, step, 0)
        if hidden % wide:
            gradient(w, whole * wide, BLOCK, 2 * whole)

    reduce_core(1)
    gradients(0)
    reduce_x(1)
    gradients(1)
    reduce_z(1)

    @pl.when(pipe < N_PIPE - 1)
    def _():
        for p in range(2):
            pipe_going[p].wait_recv()
            handed_out[p * rows : (p + 1) * rows, :] = pipe_recv[p]

    @pl.when(pipe == N_PIPE - 1)
    def _():
        handed_out[...] = jnp.zeros_like(handed_out)

    @pl.when(pipe > 0)
    def _():
        for p in range(2):
            pipe_going[p].wait_send()

    for made in sent:
        made.wait_send()


def per_device(
    activations, upstream, gate_value, up_value, hidden_grad,
    gate_weight, up_weight, gate_mask, up_mask,
):
    gate_float = gate_value[0].astype(F32)
    up_float = up_value[0].astype(F32)
    hidden_float = hidden_grad[0].astype(F32)
    gate_sigmoid = jax.nn.sigmoid(gate_float)
    up_delta = (hidden_float * gate_float * gate_sigmoid).astype(BF16)
    gate_delta = (
        hidden_float * up_float * gate_sigmoid * (1.0 + gate_float * (1.0 - gate_sigmoid))
    ).astype(BF16)
    tokens, hidden = gate_delta.shape
    width = activations.shape[2]
    rows = tokens // 4
    delta = jnp.concatenate([gate_delta, up_delta], axis=1)
    delta = delta.reshape(2, 2, rows, 2 * hidden).swapaxes(0, 1).reshape(4, rows, 2 * hidden)
    vmem = pl.BlockSpec(memory_space=pltpu.VMEM)
    smem = pl.BlockSpec(memory_space=pltpu.SMEM)
    copies = 64
    gate_gradient, up_gradient, handed = pl.pallas_call(
        kernel,
        out_shape=(
            jax.ShapeDtypeStruct((width, hidden), BF16),
            jax.ShapeDtypeStruct((width, hidden), BF16),
            jax.ShapeDtypeStruct((2 * rows, width), BF16),
        ),
        in_specs=[vmem] * 5 + [smem] * 2,
        out_specs=[vmem] * 3,
        scratch_shapes=[
            pltpu.VMEM((N_DP, 4, rows, 2 * hidden), BF16),
            pltpu.VMEM((2, CHIPS, 2 * rows, width), BF16),
            pltpu.VMEM((N_DP * 4 * rows, width), BF16),
            pltpu.VMEM((width, N_DP * 4 * rows), BF16),
            pltpu.VMEM((2 * hidden, width), BF16),
            pltpu.VMEM((2, N_DP, 2, rows, width), F32),
            pltpu.VMEM((2, N_DP, rows, width), F32),
            pltpu.VMEM((2, N_DP, rows, width), BF16),
            pltpu.VMEM((2, N_DP, rows, width), BF16),
            pltpu.VMEM((2, N_X - 1, 2, rows, width), BF16),
            pltpu.VMEM((2, N_X - 1, 2, rows, width), BF16),
            pltpu.VMEM((2, rows, width), BF16),
            pltpu.VMEM((2, rows, width), BF16),
            pltpu.VMEM((2, rows, width), BF16),
            pltpu.VMEM((2, rows, width), BF16),
            pltpu.SemaphoreType.DMA((copies,)),
            pltpu.SemaphoreType.DMA((copies,)),
            pltpu.SemaphoreType.DMA,
        ],
        compiler_params=pltpu.CompilerParams(
            collective_id=0, has_side_effects=True, vmem_limit_bytes=48 * 1024 * 1024
        ),
    )(
        delta, activations[0], upstream[0], gate_weight[0], up_weight[0], gate_mask[0], up_mask[0]
    )
    return (gate_gradient[None], up_gradient[None], handed[None])


def solution(mesh):
    return jax.shard_map(
        per_device,
        mesh=mesh,
        in_specs=(
            P("pipe", "tensor", "dp"),
            P("pipe", "tensor", "dp"),
            P("pipe", "dp", "tensor"),
            P("pipe", "dp", "tensor"),
            P("pipe", "dp", "tensor"),
            P("pipe", "dp", "tensor"),
            P("pipe", "dp", "tensor"),
            P("pipe", "dp", "tensor"),
            P("pipe", "dp", "tensor"),
        ),
        out_specs=(P("pipe", "dp", "tensor"), P("pipe", "dp", "tensor"), P("pipe", "tensor", "dp")),
        check_vma=False,
    )
```

time: 297 us -> 91.6 us (0.31)
  the two profiles are of different devices: /device:TPU:6 before, /device:TPU:88 now
where the time goes in v2:
time: 91.6 us; the launch traced here: 91.4 us
  Pallas kernels  85.3 us (93%)
  local copies, waits for them, and re-layouts  3.64 us (4%)
  other arithmetic  1.69 us (2%)
    pallas_call x1, Pallas kernels, per_device(): pl.pallas_call(kernel, out_shape=(jax.ShapeDtypeStruct((width, hidden), B...  85.3 us
    unnamed x15, local copies, waits for them, and re-layouts  3.64 us

profile of v2, /device:TPU:88, one launch (start us, length us, event | category | flops | bytes accessed | tf_op | source)
XLA Modules:
  0.0 91.4 jit_solution(15538113341645444299)
XLA Ops:
  0.6 0.0 copy-start.1
  0.6 1.6 %fusion.2 = (bf16[2,2,48,896]{3,2,0,1:T(8,128)(2,1)S(1)}, bf16[2,2,48,896]{3,2,0,1:T(8,128)(2,1)S(1)}) fusion(bf16[2,2,48,896]{3,2,1,0:T(8,128)(2,1)} %bitcast.28, bf16[2,2,48,896]{3,2,1,0:T(8,128)(2,1)} %bitcast.29, bf16[2,2,48,896]{3,2,1,0:T(8,128)(2,1)} %bitcast.30), kind=kLoop, calls=%fused_computation.4 | loop fusion | flops 2752512 | bytes 1720320 | tf_op jit(solution)/shard_map/convert_element_type | solution.py:293
  2.3 0.0 copy-start
  2.3 0.0 copy-start.2
  2.3 0.0 copy-start.3
  2.3 0.0 copy-start.4
  2.3 0.0 copy-start.5
  2.3 0.1 pad_maximum_fusion
  2.4 0.0 copy-done.1
  2.4 1.1 %copy-done = bf16[1,512,896]{2,1,0:T(8,128)(2,1)S(1)} copy-done((bf16[1,512,896]{2,1,0:T(8,128)(2,1)S(1)}, bf16[1,512,896]{2,1,0:T(8,128)(2,1)}, u32[]{:S(2)}) %copy-start) | copy-done | bytes 917528
  3.5 0.1 copy-done.2
  3.5 0.0 copy-done.3
  3.5 0.0 copy-done.4
  3.5 0.0 copy-done.5
  3.5 85.3 %shard_map.112 = (bf16[512,896]{1,0:T(8,128)(2,1)S(1)}, bf16[512,896]{1,0:T(8,128)(2,1)S(1)}, bf16[96,512]{1,0:T(8,128)(2,1)S(1)}) custom-call(bf16[4,48,1792]{2,1,0:T(8,128)(2,1)S(1)} %bitcast.18, bf16[96,512]{1,0:T(8,128)(2,1)S(1)} %bitcast.24, bf16[96,512]{1,0:T(8,128)(2,1)S(1)} %bitcast.25, bf16[512,896]{1,0:T(8,128)(2,1)S(1)} %bitcast.21, ...), custom_call_target="tpu_custom_call" | custom-call | tf_op jit(solution)/shard_map/pallas_call | solution.py:302
  88.9 0.9 %copy.32 = bf16[1,512,896]{2,1,0:T(8,128)(2,1)} copy(bf16[1,512,896]{2,1,0:T(8,128)(2,1)S(1)} %bitcast.20) | data formatting | bytes 1835008
  89.8 0.9 %copy.33 = bf16[1,512,896]{2,1,0:T(8,128)(2,1)} copy(bf16[1,512,896]{2,1,0:T(8,128)(2,1)S(1)} %bitcast.19) | data formatting | bytes 1835008
  90.7 0.6 copy.34
Async XLA Ops:
  0.6 1.8 %copy-start.1 = (bf16[1,512,896]{2,1,0:T(8,128)(2,1)S(1)}, bf16[1,512,896]{2,1,0:T(8,128)(2,1)}, u32[]{:S(2)}) copy-start(bf16[1,512,896]{2,1,0:T(8,128)(2,1)} %param.15) | copy-start | bytes 2752516
  2.3 1.2 %copy-start = (bf16[1,512,896]{2,1,0:T(8,128)(2,1)S(1)}, bf16[1,512,896]{2,1,0:T(8,128)(2,1)}, u32[]{:S(2)}) copy-start(bf16[1,512,896]{2,1,0:T(8,128)(2,1)} %param.14) | copy-start | bytes 2752516
  2.3 1.2 %copy-start.2 = (bf16[1,96,512]{2,1,0:T(8,128)(2,1)S(1)}, bf16[1,96,512]{2,1,0:T(8,128)(2,1)}, u32[]{:S(2)}) copy-start(bf16[1,96,512]{2,1,0:T(8,128)(2,1)} %param.9) | copy-start | bytes 294916
  2.3 1.2 %copy-start.3 = (bf16[1,96,512]{2,1,0:T(8,128)(2,1)S(1)}, bf16[1,96,512]{2,1,0:T(8,128)(2,1)}, u32[]{:S(2)}) copy-start(bf16[1,96,512]{2,1,0:T(8,128)(2,1)} %param.10) | copy-start | bytes 294916
  2.3 1.2 %copy-start.4 = (s32[1,4,7]{2,1,0:T(4,128)S(1)}, s32[1,4,7]{2,1,0:T(4,128)}, u32[]{:S(2)}) copy-start(s32[1,4,7]{2,1,0:T(4,128)} %param.16) | copy-start | bytes 340
  2.3 1.2 %copy-start.5 = (s32[1,4,7]{2,1,0:T(4,128)S(1)}, s32[1,4,7]{2,1,0:T(4,128)}, u32[]{:S(2)}) copy-start(s32[1,4,7]{2,1,0:T(4,128)} %param.17) | copy-start | bytes 340

commit v3 on v2

--- a/solution.py
+++ b/solution.py
@@ -11,15 +11,16 @@
 N_DP, N_X, N_PIPE = 8, 4, 4
 CHIPS = 2 * N_X
 HOPS = N_DP // 2
+THIRDS = 3
 BLOCK = 128
 
 
 def kernel(
-    delta_ref, act_ref, up_ref, gate_w, up_w, gate_mask, up_mask,
+    delta_ref, act_ref, up_ref, gate_hbm, up_hbm, gate_mask, up_mask,
     gate_out, up_out, handed_out,
     ring, act, act_rows, act_cols, kept, part, total,
     core_send, core_recv, x_send, x_recv, z_send, z_recv, pipe_send, pipe_recv,
-    send_sem, recv_sem, local_sem,
+    gate_w, up_w, send_sem, recv_sem, local_sem,
 ):
     rows, hidden2 = delta_ref.shape[1:]
     hidden = hidden2 // 2
@@ -40,6 +41,13 @@
     before = {"pipe": (pipe + N_PIPE - 1) % N_PIPE}
     after = {"pipe": (pipe + 1) % N_PIPE}
 
+    weights_in = [
+        pltpu.make_async_copy(gate_hbm, gate_w, local_sem.at[1]),
+        pltpu.make_async_copy(up_hbm, up_w, local_sem.at[2]),
+    ]
+    for made in weights_in:
+        made.start()
+
     barrier = pltpu.get_barrier_semaphore()
     greeted = [right, left, other_core, other_z, before, after] + along_x[1:]
     for other in greeted:
@@ -66,7 +74,7 @@
     going = {}
 
     def launch(d, p, h, c):
-        q = 2 * p + c
+        q = c * THIRDS + p
         if h == 1:
             src = delta_ref.at[q]
         else:
@@ -82,15 +90,16 @@
             elif d == c:
                 launch(d, p, HOPS, c)
 
-    for c in range(2):
-        for d in range(2):
-            launch(d, 0, 1, c)
+    for p in range(2):
+        for c in range(2):
+            for d in range(2):
+                launch(d, p, 1, c)
 
     act_z = start(copy(act_ref, act.at[core, chip], other_z))
     act_own = [
         start(copy(act_ref, act.at[core, chip], along_x[s])) for s in range(1, N_X)
     ]
-    home = pltpu.make_async_copy(act_ref, act.at[core, chip], local_sem)
+    home = pltpu.make_async_copy(act_ref, act.at[core, chip], local_sem.at[0])
     home.start()
 
     ring[0] = delta_ref[...]
@@ -105,6 +114,8 @@
                 kept[pl.ds(to, BLOCK), i * BLOCK : (i + 1) * BLOCK] = block.T.astype(BF16)
         return carry
 
+    for made in weights_in:
+        made.wait()
     lax.fori_loop(0, hidden // BLOCK, keep, 0)
 
     core_going = {}
@@ -114,9 +125,18 @@
 
     def multiply(p, h):
         first, n = places(h)
-        lhs = ring[first : first + n, 2 * p : 2 * p + 2].reshape(n * 2 * rows, hidden2)
+        lhs = jnp.concatenate(
+            [
+                ring[first : first + n, c * THIRDS + p].reshape(n * rows, hidden2)
+                for c in range(2)
+            ],
+            axis=0,
+        )
         out = jnp.dot(lhs, kept[...], preferred_element_type=F32)
-        part[p, first : first + n] = out.reshape(n, 2, rows, width)
+        for c in range(2):
+            part[p, first : first + n, c] = out[c * n * rows : (c + 1) * n * rows].reshape(
+                n, rows, width
+            )
         for k in range(first, first + n):
             core_send[p, k] = part[p, k, 1 - core].astype(BF16)
 
@@ -167,70 +187,82 @@
         def _():
             made.start()
 
-    multiply(0, 0)
-    send_core(0, 0)
+    def turn(k, carry):
+        at = pl.multiple_of(k * BLOCK, BLOCK)
+        act_cols[:, pl.ds(at, BLOCK)] = act_rows[pl.ds(at, BLOCK), :].astype(F32).T.astype(BF16)
+        return carry
+
+    def order_rows():
+        distance = [0, 7, 1, 6, 2, 5, 3, 4]
+        for k in range(N_DP):
+            block = (j + distance[k]) % N_DP
+            for c in range(2):
+                at = (k * 2 + c) * THIRDS * rows
+                act_rows[at : at + THIRDS * rows, :] = act[c, block]
+        lax.fori_loop(0, act_rows.shape[0] // BLOCK, turn, 0)
+
+    for p in range(2):
+        multiply(p, 0)
+        send_core(p, 0)
     for h in range(1, HOPS - 1):
-        for c in range(2):
-            arrive(0, h, c)
-        multiply(0, h)
-        send_core(0, h)
+        for p in range(2):
+            for c in range(2):
+                arrive(p, h, c)
         if h == 1:
             act_z.wait_recv()
             far = act.at[core, (1 - zh) * N_X + x]
             act_far = [start(copy(far, far, along_x[s])) for s in range(1, N_X)]
-    arrive(0, HOPS - 1, 0)
-    launch(1, 1, 1, 0)
-    arrive(0, HOPS - 1, 1)
-    launch(0, 1, 1, 0)
-    launch(0, 1, 1, 1)
-    launch(1, 1, 1, 1)
-    multiply(0, HOPS - 1)
-    send_core(0, HOPS - 1)
+        for p in range(2):
+            multiply(p, h)
+            send_core(p, h)
     for made in act_own + act_far:
         made.wait_recv()
     home.wait()
     act_core = start(copy(act.at[core], act.at[core], other_core))
+    for c in range(2):
+        arrive(0, HOPS - 1, c)
+    for d in range(2):
+        launch(d, 2, 1, 0)
+    arrive(1, HOPS - 1, 0)
+    for d in range(2):
+        launch(d, 2, 1, 1)
+    arrive(1, HOPS - 1, 1)
+    act_core.wait_recv()
+    order_rows()
+    for p in range(2):
+        multiply(p, HOPS - 1)
+        send_core(p, HOPS - 1)
+
     for d in range(2):
         going[d, 0, HOPS, d].wait_recv()
     multiply(0, HOPS)
     send_core(0, HOPS)
-
-    multiply(1, 0)
-    send_core(1, 0)
-    for c in range(2):
-        arrive(1, 1, c)
-    reduce_core(0)
-    multiply(1, 1)
-    send_core(1, 1)
-    for c in range(2):
-        arrive(1, 2, c)
-    reduce_x(0)
-    multiply(1, 2)
-    send_core(1, 2)
-    act_core.wait_recv()
-    distance = [0, 7, 1, 6, 2, 5, 3, 4]
-    for k in range(N_DP):
-        block = (j + distance[k]) % N_DP
-        for p in range(2):
-            for c in range(2):
-                at = ((k * 2 + p) * 2 + c) * rows
-                act_rows[at : at + rows, :] = act[c, block, p * rows : (p + 1) * rows, :]
-
-    def turn(k, carry):
-        at = pl.multiple_of(k * BLOCK, BLOCK)
-        act_cols[:, pl.ds(at, BLOCK)] = act_rows[pl.ds(at, BLOCK), :].astype(F32).T.astype(BF16)
-        return carry
-
-    lax.fori_loop(0, act_rows.shape[0] // BLOCK, turn, 0)
-    for c in range(2):
-        arrive(1, HOPS - 1, c)
-    multiply(1, HOPS - 1)
-    send_core(1, HOPS - 1)
-    reduce_z(0)
+    arrive(2, 1, 0)
+    arrive(2, 1, 1)
     for d in range(2):
         going[d, 1, HOPS, d].wait_recv()
     multiply(1, HOPS)
     send_core(1, HOPS)
+    reduce_core(0)
+    arrive(2, 2, 0)
+    reduce_core(1)
+    arrive(2, 2, 1)
+    multiply(2, 0)
+    send_core(2, 0)
+    multiply(2, 1)
+    send_core(2, 1)
+    arrive(2, HOPS - 1, 0)
+    reduce_x(0)
+    arrive(2, HOPS - 1, 1)
+    reduce_x(1)
+    multiply(2, 2)
+    send_core(2, 2)
+    multiply(2, HOPS - 1)
+    send_core(2, HOPS - 1)
+    for d in range(2):
+        going[d, 2, HOPS, d].wait_recv()
+    multiply(2, HOPS)
+    send_core(2, HOPS)
 
     def gradient(w, at, wide, first_block):
         out, mask = ((gate_out, gate_mask), (up_out, up_mask))[w]
@@ -254,15 +286,17 @@
         if hidden % wide:
             gradient(w, whole * wide, BLOCK, 2 * whole)
 
-    reduce_core(1)
+    reduce_core(2)
+    reduce_z(0)
+    reduce_z(1)
     gradients(0)
-    reduce_x(1)
+    reduce_x(2)
     gradients(1)
-    reduce_z(1)
+    reduce_z(2)
 
     @pl.when(pipe < N_PIPE - 1)
     def _():
-        for p in range(2):
+        for p in range(THIRDS):
             pipe_going[p].wait_recv()
             handed_out[p * rows : (p + 1) * rows, :] = pipe_recv[p]
 
@@ -272,7 +306,7 @@
 
     @pl.when(pipe > 0)
     def _():
-        for p in range(2):
+        for p in range(THIRDS):
             pipe_going[p].wait_send()
 
     for made in sent:
@@ -293,43 +327,45 @@
     ).astype(BF16)
     tokens, hidden = gate_delta.shape
     width = activations.shape[2]
-    rows = tokens // 4
+    rows = tokens // (2 * THIRDS)
     delta = jnp.concatenate([gate_delta, up_delta], axis=1)
-    delta = delta.reshape(2, 2, rows, 2 * hidden).swapaxes(0, 1).reshape(4, rows, 2 * hidden)
+    delta = delta.reshape(2 * THIRDS, rows, 2 * hidden)
     vmem = pl.BlockSpec(memory_space=pltpu.VMEM)
     smem = pl.BlockSpec(memory_space=pltpu.SMEM)
-    copies = 64
+    copies = 80
     gate_gradient, up_gradient, handed = pl.pallas_call(
         kernel,
         out_shape=(
             jax.ShapeDtypeStruct((width, hidden), BF16),
             jax.ShapeDtypeStruct((width, hidden), BF16),
-            jax.ShapeDtypeStruct((2 * rows, width), BF16),
+            jax.ShapeDtypeStruct((THIRDS * rows, width), BF16),
         ),
-        in_specs=[vmem] * 5 + [smem] * 2,
+        in_specs=[vmem] * 3 + [pl.BlockSpec(memory_space=pltpu.HBM)] * 2 + [smem] * 2,
         out_specs=[vmem] * 3,
         scratch_shapes=[
-            pltpu.VMEM((N_DP, 4, rows, 2 * hidden), BF16),
-            pltpu.VMEM((2, CHIPS, 2 * rows, width), BF16),
-            pltpu.VMEM((N_DP * 4 * rows, width), BF16),
-            pltpu.VMEM((width, N_DP * 4 * rows), BF16),
+            pltpu.VMEM((N_DP, 2 * THIRDS, rows, 2 * hidden), BF16),
+            pltpu.VMEM((2, CHIPS, THIRDS * rows, width), BF16),
+            pltpu.VMEM((N_DP * 2 * THIRDS * rows, width), BF16),
+            pltpu.VMEM((width, N_DP * 2 * THIRDS * rows), BF16),
             pltpu.VMEM((2 * hidden, width), BF16),
-            pltpu.VMEM((2, N_DP, 2, rows, width), F32),
-            pltpu.VMEM((2, N_DP, rows, width), F32),
-            pltpu.VMEM((2, N_DP, rows, width), BF16),
-            pltpu.VMEM((2, N_DP, rows, width), BF16),
-            pltpu.VMEM((2, N_X - 1, 2, rows, width), BF16),
-            pltpu.VMEM((2, N_X - 1, 2, rows, width), BF16),
-            pltpu.VMEM((2, rows, width), BF16),
-            pltpu.VMEM((2, rows, width), BF16),
-            pltpu.VMEM((2, rows, width), BF16),
-            pltpu.VMEM((2, rows, width), BF16),
+            pltpu.VMEM((THIRDS, N_DP, 2, rows, width), F32),
+            pltpu.VMEM((THIRDS, N_DP, rows, width), F32),
+            pltpu.VMEM((THIRDS, N_DP, rows, width), BF16),
+            pltpu.VMEM((THIRDS, N_DP, rows, width), BF16),
+            pltpu.VMEM((THIRDS, N_X - 1, 2, rows, width), BF16),
+            pltpu.VMEM((THIRDS, N_X - 1, 2, rows, width), BF16),
+            pltpu.VMEM((THIRDS, rows, width), BF16),
+            pltpu.VMEM((THIRDS, rows, width), BF16),
+            pltpu.VMEM((THIRDS, rows, width), BF16),
+            pltpu.VMEM((THIRDS, rows, width), BF16),
+            pltpu.VMEM((width, hidden), BF16),
+            pltpu.VMEM((width, hidden), BF16),
             pltpu.SemaphoreType.DMA((copies,)),
             pltpu.SemaphoreType.DMA((copies,)),
-            pltpu.SemaphoreType.DMA,
+            pltpu.SemaphoreType.DMA((3,)),
         ],
         compiler_params=pltpu.CompilerParams(
-            collective_id=0, has_side_effects=True, vmem_limit_bytes=48 * 1024 * 1024
+            collective_id=0, has_side_effects=True, vmem_limit_bytes=40 * 1024 * 1024
         ),
     )(
         delta, activations[0], upstream[0], gate_weight[0], up_weight[0], gate_mask[0], up_mask[0]

time: 91.6 us -> 90.7 us (level)
  the two profiles are of different devices: /device:TPU:88 before, /device:TPU:6 now
where the time goes in v3:
time: 90.7 us; the launch traced here: 89.6 us
  Pallas kernels  83.6 us (92%)
  local copies, waits for them, and re-layouts  3.65 us (4%)
  other arithmetic  1.69 us (2%)
    pallas_call x1, Pallas kernels, per_device(): pl.pallas_call(kernel, out_shape=(jax.ShapeDtypeStruct((width, hidden), B...  83.6 us
    unnamed x15, local copies, waits for them, and re-layouts  3.65 us

profile of v3, /device:TPU:6, one launch (start us, length us, event | category | flops | bytes accessed | tf_op | source)
XLA Modules:
  0.0 89.6 jit_solution(18242359433205188570)
XLA Ops:
  0.6 0.0 copy-start.1
  0.6 1.6 %fusion.2 = (bf16[6,32,896]{2,1,0:T(8,128)(2,1)S(1)}, bf16[6,32,896]{2,1,0:T(8,128)(2,1)S(1)}) fusion(bf16[6,32,896]{2,1,0:T(8,128)(2,1)} %bitcast.24, bf16[6,32,896]{2,1,0:T(8,128)(2,1)} %bitcast.25, bf16[6,32,896]{2,1,0:T(8,128)(2,1)} %bitcast.26), kind=kLoop, calls=%fused_computation.6 | loop fusion | flops 2752512 | bytes 1720320 | tf_op jit(solution)/shard_map/convert_element_type | solution.py:327
  2.3 0.0 copy-start
  2.3 0.0 copy-start.2
  2.3 0.0 copy-start.3
  2.3 0.0 copy-start.4
  2.3 0.0 copy-start.5
  2.3 0.1 pad_maximum_fusion.delta_ref
  2.4 0.0 copy-done.1
  2.4 1.1 %copy-done = bf16[1,512,896]{2,1,0:T(8,128)(2,1)S(1)} copy-done((bf16[1,512,896]{2,1,0:T(8,128)(2,1)S(1)}, bf16[1,512,896]{2,1,0:T(8,128)(2,1)}, u32[]{:S(2)}) %copy-start) | copy-done | bytes 917528
  3.5 0.1 copy-done.2
  3.5 0.0 copy-done.3
  3.5 0.0 copy-done.4
  3.5 0.0 copy-done.5
  3.5 83.6 %shard_map.112 = (bf16[512,896]{1,0:T(8,128)(2,1)S(1)}, bf16[512,896]{1,0:T(8,128)(2,1)S(1)}, bf16[96,512]{1,0:T(8,128)(2,1)S(1)}) custom-call(bf16[6,32,1792]{2,1,0:T(8,128)(2,1)S(1)} %pad_maximum_fusion.delta_ref, bf16[96,512]{1,0:T(8,128)(2,1)S(1)} %bitcast.20, bf16[96,512]{1,0:T(8,128)(2,1)S(1)} %bitcast.21, bf16[512,896]{1,0:T(8,128)(2,1)S(1)} %bitcast.17, ...), custom_call_target="tpu_custom_call" | custom-call | tf_op jit(solution)/shard_map/pallas_call | solution.py:336
  87.1 0.9 %copy.15 = bf16[1,512,896]{2,1,0:T(8,128)(2,1)} copy(bf16[1,512,896]{2,1,0:T(8,128)(2,1)S(1)} %bitcast.16) | data formatting | bytes 1835008
  88.1 0.9 %copy.16 = bf16[1,512,896]{2,1,0:T(8,128)(2,1)} copy(bf16[1,512,896]{2,1,0:T(8,128)(2,1)S(1)} %bitcast.15) | data formatting | bytes 1835008
  89.0 0.6 copy.17
Async XLA Ops:
  0.6 1.8 %copy-start.1 = (bf16[1,512,896]{2,1,0:T(8,128)(2,1)S(1)}, bf16[1,512,896]{2,1,0:T(8,128)(2,1)}, u32[]{:S(2)}) copy-start(bf16[1,512,896]{2,1,0:T(8,128)(2,1)} %param.15) | copy-start | bytes 2752516
  2.3 1.2 %copy-start = (bf16[1,512,896]{2,1,0:T(8,128)(2,1)S(1)}, bf16[1,512,896]{2,1,0:T(8,128)(2,1)}, u32[]{:S(2)}) copy-start(bf16[1,512,896]{2,1,0:T(8,128)(2,1)} %param.14) | copy-start | bytes 2752516
  2.3 1.2 %copy-start.2 = (bf16[1,96,512]{2,1,0:T(8,128)(2,1)S(1)}, bf16[1,96,512]{2,1,0:T(8,128)(2,1)}, u32[]{:S(2)}) copy-start(bf16[1,96,512]{2,1,0:T(8,128)(2,1)} %param.9) | copy-start | bytes 294916
  2.3 1.2 %copy-start.3 = (bf16[1,96,512]{2,1,0:T(8,128)(2,1)S(1)}, bf16[1,96,512]{2,1,0:T(8,128)(2,1)}, u32[]{:S(2)}) copy-start(bf16[1,96,512]{2,1,0:T(8,128)(2,1)} %param.10) | copy-start | bytes 294916
  2.3 1.2 %copy-start.4 = (s32[1,4,7]{2,1,0:T(4,128)S(1)}, s32[1,4,7]{2,1,0:T(4,128)}, u32[]{:S(2)}) copy-start(s32[1,4,7]{2,1,0:T(4,128)} %param.16) | copy-start | bytes 340
  2.3 1.2 %copy-start.5 = (s32[1,4,7]{2,1,0:T(4,128)S(1)}, s32[1,4,7]{2,1,0:T(4,128)}, u32[]{:S(2)}) copy-start(s32[1,4,7]{2,1,0:T(4,128)} %param.17) | copy-start | bytes 340

commit v4 on v3

--- a/solution.py
+++ b/solution.py
@@ -365,7 +365,7 @@
             pltpu.SemaphoreType.DMA((3,)),
         ],
         compiler_params=pltpu.CompilerParams(
-            collective_id=0, has_side_effects=True, vmem_limit_bytes=40 * 1024 * 1024
+            collective_id=0, has_side_effects=True, vmem_limit_bytes=51 * 1024 * 1024
         ),
     )(
         delta, activations[0], upstream[0], gate_weight[0], up_weight[0], gate_mask[0], up_mask[0]

time: 90.7 us -> 89.9 us (level)
    unnamed x15 -> x11, local copies, waits for them, and re-layouts: 3.65 us -> 3.35 us
where the time goes in v4:
time: 89.9 us; the launch traced here: 88.8 us
  Pallas kernels  83.1 us (92%)
  local copies, waits for them, and re-layouts  3.35 us (4%)
  other arithmetic  1.61 us (2%)
    pallas_call x1, Pallas kernels, per_device(): pl.pallas_call(kernel, out_shape=(jax.ShapeDtypeStruct((width, hidden), B...  83.1 us
    unnamed x11, local copies, waits for them, and re-layouts  3.35 us

profile of v4, /device:TPU:6, one launch (start us, length us, event | category | flops | bytes accessed | tf_op | source)
XLA Modules:
  0.0 88.8 jit_solution(17941527195204060162)
XLA Ops:
  0.6 1.6 %fusion.2 = (bf16[6,32,896]{2,1,0:T(8,128)(2,1)S(1)}, bf16[6,32,896]{2,1,0:T(8,128)(2,1)S(1)}) fusion(bf16[6,32,896]{2,1,0:T(8,128)(2,1)} %bitcast.24, bf16[6,32,896]{2,1,0:T(8,128)(2,1)} %bitcast.25, bf16[6,32,896]{2,1,0:T(8,128)(2,1)} %bitcast.26), kind=kLoop, calls=%fused_computation.6 | loop fusion | flops 2752512 | bytes 1720320 | tf_op jit(solution)/shard_map/convert_element_type | solution.py:327
  2.2 0.0 copy-start
  2.2 0.0 copy-start.1
  2.2 0.0 copy-start.2
  2.2 0.0 copy-start.3
  2.2 0.1 pad_maximum_fusion.delta_ref
  2.3 0.8 copy-done
  3.1 0.0 copy-done.1
  3.1 0.0 copy-done.2
  3.1 0.0 copy-done.3
  3.1 83.1 %shard_map.112 = (bf16[512,896]{1,0:T(8,128)(2,1)S(1)}, bf16[512,896]{1,0:T(8,128)(2,1)S(1)}, bf16[96,512]{1,0:T(8,128)(2,1)S(1)}) custom-call(bf16[6,32,1792]{2,1,0:T(8,128)(2,1)S(1)} %pad_maximum_fusion.delta_ref, bf16[96,512]{1,0:T(8,128)(2,1)S(1)} %bitcast.18, bf16[96,512]{1,0:T(8,128)(2,1)S(1)} %bitcast.19, bf16[512,896]{1,0:T(8,128)(2,1)} %bitcast.22, ...), custom_call_target="tpu_custom_call" | custom-call | tf_op jit(solution)/shard_map/pallas_call | solution.py:336
  86.3 0.9 %copy.15 = bf16[1,512,896]{2,1,0:T(8,128)(2,1)} copy(bf16[1,512,896]{2,1,0:T(8,128)(2,1)S(1)} %bitcast.16) | data formatting | bytes 1835008
  87.2 0.9 %copy.16 = bf16[1,512,896]{2,1,0:T(8,128)(2,1)} copy(bf16[1,512,896]{2,1,0:T(8,128)(2,1)S(1)} %bitcast.15) | data formatting | bytes 1835008
  88.1 0.6 copy.17
Async XLA Ops:
  2.2 0.9 %copy-start = (bf16[1,96,512]{2,1,0:T(8,128)(2,1)S(1)}, bf16[1,96,512]{2,1,0:T(8,128)(2,1)}, u32[]{:S(2)}) copy-start(bf16[1,96,512]{2,1,0:T(8,128)(2,1)} %param.9) | copy-start | bytes 294916
  2.2 0.9 %copy-start.1 = (bf16[1,96,512]{2,1,0:T(8,128)(2,1)S(1)}, bf16[1,96,512]{2,1,0:T(8,128)(2,1)}, u32[]{:S(2)}) copy-start(bf16[1,96,512]{2,1,0:T(8,128)(2,1)} %param.10) | copy-start | bytes 294916
  2.2 0.9 %copy-start.2 = (s32[1,4,7]{2,1,0:T(4,128)S(1)}, s32[1,4,7]{2,1,0:T(4,128)}, u32[]{:S(2)}) copy-start(s32[1,4,7]{2,1,0:T(4,128)} %param.16) | copy-start | bytes 340
  2.2 0.9 %copy-start.3 = (s32[1,4,7]{2,1,0:T(4,128)S(1)}, s32[1,4,7]{2,1,0:T(4,128)}, u32[]{:S(2)}) copy-start(s32[1,4,7]{2,1,0:T(4,128)} %param.17) | copy-start | bytes 340
